TPU v7x, 32 devices: a whole 2x2x4 slice. The times are simulated.
32 devices in a mesh: cfg: 2 (over y), space: 4 (over z), tm: 4 (over x, core).
Axes of the slice: x: 2, y: 2, z: 4, core: 2. Of those that a mesh axis runs over, the one named last changes fastest.
Arguments:
- eigenvectors: bfloat16 [8, 2, 3, 3072, 384], P(('cfg', 'tm'), None, None, 'space'), parts along dimension 0, may hold values from -6 to 6
- perambulator: bfloat16 [8, 2, 1536, 1536], P(('cfg', 'tm'), None, None, 'space'), parts along dimension 0, may hold values from -0.3125 to 0.3125
- momenta: int32 [2, 3], replicated, may hold values from -2 to 2
- ratios: int32 [2, 2], replicated, may hold values from 1 to 3
- source_slice: int32 [1], replicated, may hold values from 0 to 255
Outputs:
- meson_blocks: float32 [8, 2, 1536, 1536], P(('cfg', 'tm'), None, 'space'), parts along dimension 0
There are 2 independent parts, one for each index of `cfg`. A program takes and returns all parts, laid end to end along the dimension named above; an argument that names none is the same for every part. Nothing has to cross between parts.
Inputs may be any that keep to these rules, and one draw needn't show every extreme that they name: `momenta`: row k is momentum k in units of 2 pi / 64. `ratios`: row k holds the numerator (column 0) and the denominator (column 1) of momentum k's coefficient.
All inputs are finite; a program needn't handle non-finite values.
Results may differ from a plain program's by a relative error of at most 0.0063.
Values may be sent and summed in bfloat16 or wider, within the bound.
A program may use at most 64 MiB of HBM per device.

v0:
```python
import functools
import math

import jax
import jax.numpy as jnp
from jax import lax
from jax.experimental import pallas as pl
from jax.experimental.pallas import tpu as pltpu
from jax.sharding import PartitionSpec as P

MESH = pl.DeviceIdType.MESH

LSIDE = 64


def spread(value, axis, source):
    kept = jnp.where(lax.axis_index(axis) == source, value, 0).astype(value.dtype)
    return lax.psum(kept, axis)


def site_phases(momenta, first_site, site_count):
    site_index = first_site + lax.iota(jnp.int32, site_count)
    along_x = site_index % LSIDE
    along_y = site_index // LSIDE % LSIDE
    along_z = site_index // (LSIDE * LSIDE)
    turn_count = (
        momenta[:, 0:1] * along_x[None, :]
        + momenta[:, 1:2] * along_y[None, :]
        + momenta[:, 2:3] * along_z[None, :]
    )
    phase_angle = (turn_count % LSIDE).astype(jnp.float32) * (2.0 * math.pi / LSIDE)
    return (jnp.cos(phase_angle), jnp.sin(phase_angle))


def split_elementals(product, vector_count):
    lead_shape = product.shape[:-2]
    product_grid = product.reshape(lead_shape + (2, vector_count, 2, 2, vector_count))
    real_part = product_grid[..., 0, :, :, 0, :] + product_grid[..., 1, :, :, 1, :]
    imaginary = product_grid[..., 0, :, :, 1, :] - product_grid[..., 1, :, :, 0, :]
    stacked = jnp.stack([real_part, imaginary], axis=-4)
    return jnp.moveaxis(stacked, -2, -4)


def elementals(vectors, cosine, sine_part):
    slab_count, color_count, site_count, vector_count = (
        vectors.shape[0],
        vectors.shape[2],
        vectors.shape[3],
        vectors.shape[4],
    )
    row_count = color_count * site_count
    real_rows = vectors[:, 0].reshape(slab_count, row_count, vector_count)
    imaginary_rows = vectors[:, 1].reshape(slab_count, row_count, vector_count)
    cos_rows = jnp.broadcast_to(cosine[:, None, :], (2, color_count, site_count)).reshape(
        1, 2, row_count, 1
    )
    sin_rows = jnp.broadcast_to(sine_part[:, None, :], (2, color_count, site_count)).reshape(
        1, 2, row_count, 1
    )
    phased_real = (cos_rows * real_rows[:, None] + sin_rows * imaginary_rows[:, None]).astype(
        jnp.bfloat16
    )
    phased_imaginary = (cos_rows * imaginary_rows[:, None] - sin_rows * real_rows[:, None]).astype(
        jnp.bfloat16
    )
    phased = jnp.concatenate([phased_real, phased_imaginary], axis=3)
    phased = jnp.transpose(phased, (0, 2, 1, 3)).reshape(slab_count, row_count, 4 * vector_count)
    plain_vectors = jnp.concatenate([real_rows, imaginary_rows], axis=2)
    product = lax.dot_general(
        plain_vectors, phased, (((1,), (1,)), ((0,), (0,))), preferred_element_type=jnp.float32
    )
    return split_elementals(product, vector_count)


def source_block(chosen):
    real_t = chosen[0].T
    imaginary_t = chosen[1].T
    upper = jnp.concatenate([real_t, -imaginary_t], axis=1)
    lower = jnp.concatenate([imaginary_t, real_t], axis=1)
    return jnp.concatenate([upper, lower], axis=0)


def propagate(sink_matrix, tau):
    vector_count = sink_matrix.shape[1]
    spin_count = tau.shape[1] // vector_count
    column_count = tau.shape[2]
    real_part, imaginary = (sink_matrix[0], sink_matrix[1])
    upper = jnp.concatenate([real_part, -imaginary], axis=1)
    lower = jnp.concatenate([imaginary, real_part], axis=1)
    sink_big = jnp.concatenate([upper, lower], axis=0)
    stacked = jnp.transpose(tau.reshape(2, spin_count, vector_count, column_count), (0, 2, 1, 3))
    stacked = stacked.reshape(2 * vector_count, spin_count * column_count)
    product = jnp.dot(sink_big, stacked, preferred_element_type=jnp.float32)
    product = jnp.transpose(
        product.reshape(2, vector_count, spin_count, column_count), (0, 2, 1, 3)
    )
    return product.reshape(2, spin_count * vector_count, column_count).astype(jnp.bfloat16)


def attach_source(propagated, source_big):
    vector_count = source_big.shape[0] // 2
    row_count = propagated.shape[1]
    spin_count = propagated.shape[2] // vector_count
    stacked = jnp.concatenate(
        [
            propagated[0].reshape(row_count, spin_count, vector_count),
            propagated[1].reshape(row_count, spin_count, vector_count),
        ],
        axis=2,
    )
    product = jnp.dot(
        stacked.reshape(row_count * spin_count, 2 * vector_count),
        source_big,
        preferred_element_type=jnp.float32,
    )
    product = jnp.transpose(product.reshape(row_count, spin_count, 2, vector_count), (2, 0, 1, 3))
    return product.reshape(2, row_count, spin_count * vector_count)


def general_body(eigenvectors, perambulator, momenta, ratios, source_slice):
    slab_count = eigenvectors.shape[0]
    color_count = eigenvectors.shape[2]
    site_count = eigenvectors.shape[3]
    vector_count = eigenvectors.shape[4]
    first_site = lax.axis_index("space") * site_count
    cosine, sine_part = site_phases(momenta, first_site, site_count)
    normalizer = 1.0 / math.sqrt(color_count * site_count * lax.axis_size("space") * vector_count)
    weights = (
        ratios[:, 0].astype(jnp.float32) / ratios[:, 1].astype(jnp.float32) * normalizer
    ).reshape(1, 2, 1, 1, 1)
    parts = elementals(eigenvectors, cosine, sine_part)
    partial_sums = jnp.sum(weights * parts, axis=1, keepdims=True)
    summed = lax.psum(partial_sums, "space")
    sink_matrices = summed[:, 0].astype(jnp.bfloat16)
    global_slice = source_slice[0] % (slab_count * lax.axis_size("tm"))
    local_source = lax.dynamic_index_in_dim(
        sink_matrices, global_slice % slab_count, 0, keepdims=False
    )
    chosen = spread(local_source, "tm", global_slice // slab_count)
    source_big = source_block(chosen)
    propagated = jnp.stack([propagate(sink_matrices[0], perambulator[0])])
    return jnp.stack(
        [
            attach_source(
                lax.all_to_all(propagated, "space", split_axis=2, concat_axis=3, tiled=True)[0],
                source_big,
            )
        ]
    )


def block_dot(left, right, left_dim, right_dim):
    return lax.dot_general(
        left, right, (((left_dim,), (right_dim,)), ((), ())), preferred_element_type=jnp.float32
    )


def exchange_kernel(
    momenta_ref,
    ratio_ref,
    slice_ref,
    eig_hbm,
    tau_hbm,
    prop_ref,
    source_ref,
    eig,
    acc,
    tau,
    part,
    pair_out,
    pair_in,
    cross_out,
    cross_in,
    sink,
    sink_pair,
    picked,
    far,
    sink_big,
    cosines,
    sines,
    eig_sem,
    own_sem,
    tau_send,
    tau_recv,
    pair_send,
    pair_recv,
    cross_send,
    cross_recv,
    back_send,
    back_recv,
    spread_send,
    spread_recv,
    *,
    normalizer,
):
    vector_count = eig_hbm.shape[4]
    site_count = eig_hbm.shape[3]
    chunk_count, chunk_rows = part.shape[0], part.shape[2]
    step_count, site_step = eig.shape[0], eig.shape[2]
    steps_per_color = site_count // site_step
    me = lax.axis_index("space")
    slot = lax.axis_index("tm")
    near = me + 1 - 2 * (me % 2)
    across = me + 2 - 4 * (me // 2)
    mirror = 3 - me
    inner = ((me + 1) // 2) % 2
    core = slot % 2
    core_peer = slot + 1 - 2 * core
    chip_peer = slot + 2 - 4 * (slot // 2)

    def eig_copy(step):
        color, first = step // steps_per_color, (step % steps_per_color) * site_step
        return pltpu.make_async_copy(
            eig_hbm.at[0, :, color, pl.ds(first, site_step), :], eig.at[step], eig_sem.at[step]
        )

    for step in range(step_count):
        eig_copy(step).start()
    own_copy = pltpu.make_async_copy(
        tau_hbm.at[0, :, pl.ds(me * vector_count, vector_count), :], tau.at[me], own_sem
    )

    barrier = pltpu.get_barrier_semaphore()
    for peer in (near, across, mirror):
        pl.semaphore_signal(barrier, inc=1, device_id={"space": peer}, device_id_type=MESH)
    for peer in (core_peer, chip_peer):
        pl.semaphore_signal(barrier, inc=1, device_id={"tm": peer}, device_id_type=MESH)
    pl.semaphore_wait(barrier, 5)

    def tau_copy(index, to, piece):
        return pltpu.make_async_remote_copy(
            src_ref=tau_hbm.at[0, piece, pl.ds(to * vector_count, vector_count), :],
            dst_ref=tau.at[me, piece],
            send_sem=tau_send.at[index, piece],
            recv_sem=tau_recv.at[me, piece],
            device_id={"space": to},
            device_id_type=MESH,
        )

    def hop(from_ref, to_ref, send_sem, recv_sem, peer):
        return pltpu.make_async_remote_copy(
            src_ref=from_ref,
            dst_ref=to_ref,
            send_sem=send_sem,
            recv_sem=recv_sem,
            device_id=peer,
            device_id_type=MESH,
        )

    near_copies = [tau_copy(0, near, piece) for piece in range(2)]
    across_copies = [tau_copy(1, across, piece) for piece in range(2)]
    mirror_copies = [tau_copy(2, mirror, piece) for piece in range(2)]

    @pl.when(inner == 1)
    def _():
        mirror_copies[0].start()
        mirror_copies[1].start()
        across_copies[0].start()

    near_copies[0].start()
    near_copies[1].start()
    own_copy.start()

    lanes = cosines.shape[1]
    site = me * site_count + lax.broadcasted_iota(jnp.int32, (site_count, lanes), 0)
    first_lane = lax.broadcasted_iota(jnp.int32, (site_count, lanes), 1) == 0
    shift = LSIDE.bit_length() - 1
    places = (
        jnp.bitwise_and(site, LSIDE - 1),
        jnp.bitwise_and(jnp.right_shift(site, shift), LSIDE - 1),
        jnp.right_shift(site, 2 * shift),
    )
    turn = jnp.zeros_like(site)
    for axis in range(3):
        turn += jnp.where(first_lane, momenta_ref[0, axis], momenta_ref[1, axis]) * places[axis]
    angle = jnp.bitwise_and(turn, LSIDE - 1).astype(jnp.float32) * (2.0 * math.pi / LSIDE)
    cosines[...] = jnp.cos(angle)
    sines[...] = jnp.sin(angle)

    acc[...] = jnp.zeros_like(acc)

    def accumulate(step, carry):
        eig_copy(step).wait()
        rows = pl.ds(pl.multiple_of((step % steps_per_color) * site_step, site_step), site_step)
        plain_real, plain_imag = eig[step, 0], eig[step, 1]
        real = plain_real.astype(jnp.float32)
        imag = plain_imag.astype(jnp.float32)
        upper, lower = [], []
        for k in range(2):
            cosine = cosines[rows, k : k + 1]
            sine = sines[rows, k : k + 1]
            turned_real = (cosine * real + sine * imag).astype(jnp.bfloat16)
            turned_imag = (cosine * imag - sine * real).astype(jnp.bfloat16)
            upper += [turned_real, turned_imag]
            lower += [turned_imag, -turned_real]
        left = jnp.concatenate([plain_real, plain_imag], axis=0)
        right = jnp.concatenate(
            [jnp.concatenate(upper, axis=1), jnp.concatenate(lower, axis=1)], axis=0
        )
        acc[...] += block_dot(left, right, 0, 0)
        return carry

    lax.fori_loop(0, step_count, accumulate, 0)

    weights = [
        jnp.full((1, vector_count), ratio_ref[k, 0], jnp.int32).astype(jnp.float32)
        / jnp.full((1, vector_count), ratio_ref[k, 1], jnp.int32).astype(jnp.float32)
        * normalizer
        for k in range(2)
    ]

    def weighted(chunk, c):
        rows = pl.ds(chunk * chunk_rows, chunk_rows)
        return (
            weights[0] * acc[rows, c * vector_count : (c + 1) * vector_count]
            + weights[1] * acc[rows, (2 + c) * vector_count : (3 + c) * vector_count]
        )

    pair_hops = [
        hop(
            pair_out.at[q], pair_in.at[q], pair_send.at[q], pair_recv.at[q], {"space": near}
        )
        for q in range(chunk_count)
    ]
    cross_hops = [
        hop(
            cross_out.at[q], cross_in.at[q], cross_send.at[q], cross_recv.at[q], {"space": mirror}
        )
        for q in range(chunk_count)
    ]
    back_hops = [
        hop(sink.at[q], sink.at[q], back_send.at[q], back_recv.at[q], {"space": near})
        for q in range(chunk_count)
    ]

    @pl.when(inner == 0)
    def _():
        for q in range(chunk_count):
            for c in range(2):
                pair_out[q, c] = weighted(q, c).astype(jnp.bfloat16)
            pair_hops[q].start()
        for q in range(chunk_count // 2):
            back_hops[q].wait_recv()
        for copy in across_copies + mirror_copies:
            copy.start()
        for q in range(chunk_count // 2, chunk_count):
            back_hops[q].wait_recv()
        for q in range(chunk_count):
            pair_hops[q].wait_send()

    @pl.when(inner == 1)
    def _():
        for q in range(chunk_count):
            for c in range(2):
                part[q, c] = weighted(q, c)
        for q in range(chunk_count):
            pair_hops[q].wait_recv()
            part[q] = part[q] + pair_in[q].astype(jnp.float32)
            cross_out[q] = part[q].astype(jnp.bfloat16)
            cross_hops[q].start()
        across_copies[1].start()
        for q in range(chunk_count):
            cross_hops[q].wait_recv()
            sink[q] = (part[q] + cross_in[q].astype(jnp.float32)).astype(jnp.bfloat16)
            back_hops[q].start()
        for q in range(chunk_count):
            cross_hops[q].wait_send()
            back_hops[q].wait_send()

    core_hop = hop(sink, sink_pair, spread_send.at[0], spread_recv.at[0], {"tm": core_peer})
    core_hop.start()
    for q in range(chunk_count):
        rows = pl.ds(q * chunk_rows, chunk_rows)
        low = pl.ds(vector_count + q * chunk_rows, chunk_rows)
        real, imag = sink[q, 0], sink[q, 1]
        sink_big[rows, :vector_count] = real
        sink_big[rows, vector_count:] = -imag
        sink_big[low, :vector_count] = imag
        sink_big[low, vector_count:] = real
    core_hop.wait()
    chosen_slot = slice_ref[0] % lax.axis_size("tm")
    picked[...] = jnp.where(chosen_slot == slot, sink[...], sink_pair[...])
    half = pl.ds(core * (chunk_count // 2), chunk_count // 2)
    chip_hop = hop(
        picked.at[half], far.at[half], spread_send.at[1], spread_recv.at[1], {"tm": chip_peer}
    )
    chip_hop.start()

    def carry_block(origin):
        stacked = tau[origin].reshape(2 * vector_count, vector_count)
        product = block_dot(sink_big[...], stacked, 1, 0).astype(jnp.bfloat16)
        prop_ref[origin, :, :vector_count] = product[:vector_count]
        prop_ref[origin, :, vector_count:] = product[vector_count:]

    def arrived(origin):
        for piece in range(2):
            hop(
                tau.at[origin, piece],
                tau.at[origin, piece],
                tau_send.at[0, piece],
                tau_recv.at[origin, piece],
                {"space": origin},
            ).wait_recv()

    own_copy.wait()
    carry_block(me)
    chip_hop.wait()
    forward_hop = hop(
        far.at[half], far.at[half], spread_send.at[2], spread_recv.at[2], {"tm": core_peer}
    )
    forward_hop.start()
    forward_hop.wait()
    chosen = jnp.where(chosen_slot // 2 == slot // 2, picked[...], far[...])
    for q in range(chunk_count):
        rows = pl.ds(q * chunk_rows, chunk_rows)
        low = pl.ds(vector_count + q * chunk_rows, chunk_rows)
        source_ref[rows, :vector_count] = chosen[q, 0]
        source_ref[rows, vector_count:] = chosen[q, 1]
        source_ref[low, :vector_count] = -chosen[q, 1]
        source_ref[low, vector_count:] = chosen[q, 0]
    for origin in (near, across, mirror):
        arrived(origin)
        carry_block(origin)
    for copy in near_copies + across_copies + mirror_copies:
        copy.wait_send()


def finish_kernel(prop_ref, source_ref, out_ref):
    vector_count = source_ref.shape[0] // 2
    product = block_dot(prop_ref[0], source_ref[...], 1, 1)
    out_ref[0, 0] = product[:, :vector_count]
    out_ref[0, 1] = product[:, vector_count:]


def body(eigenvectors, perambulator, momenta, ratios, source_slice):
    color_count, site_count, vector_count = eigenvectors.shape[2:]
    group = lax.axis_size("space")
    normalizer = 1.0 / math.sqrt(color_count * site_count * group * vector_count)
    site_step = site_count // 2
    step_count = 2 * color_count
    chunk_count = 4
    whole = (chunk_count, 2, vector_count // chunk_count, vector_count)
    bf16, f32 = jnp.bfloat16, jnp.float32
    smem = pl.BlockSpec(memory_space=pltpu.SMEM)
    vmem = pl.BlockSpec(memory_space=pltpu.VMEM)
    anywhere = pl.BlockSpec(memory_space=pl.ANY)
    dma = pltpu.SemaphoreType.DMA
    propagated, source_big = pl.pallas_call(
        functools.partial(exchange_kernel, normalizer=normalizer),
        out_shape=(
            jax.ShapeDtypeStruct((group, vector_count, 2 * vector_count), bf16),
            jax.ShapeDtypeStruct((2 * vector_count, 2 * vector_count), bf16),
        ),
        in_specs=[smem, smem, smem, anywhere, anywhere],
        out_specs=(vmem, vmem),
        scratch_shapes=[
            pltpu.VMEM((step_count, 2, site_step, vector_count), bf16),
            pltpu.VMEM((vector_count, 4 * vector_count), f32),
            pltpu.VMEM((group, 2, vector_count, vector_count), bf16),
            pltpu.VMEM(whole, f32),
            *[pltpu.VMEM(whole, bf16) for _ in range(8)],
            pltpu.VMEM((2 * vector_count, 2 * vector_count), bf16),
            pltpu.VMEM((site_count, 128), f32),
            pltpu.VMEM((site_count, 128), f32),
            dma((step_count,)),
            dma,
            dma((3, 2)),
            dma((group, 2)),
            *[dma((chunk_count,)) for _ in range(6)],
            dma((3,)),
            dma((3,)),
        ],
        compiler_params=pltpu.CompilerParams(collective_id=0, has_side_effects=True),
        name="exchange",
    )(momenta, ratios, source_slice, eigenvectors, perambulator)
    return pl.pallas_call(
        finish_kernel,
        grid=(group,),
        out_shape=jax.ShapeDtypeStruct((1, 2, vector_count, group * vector_count), f32),
        in_specs=[
            pl.BlockSpec((1, vector_count, 2 * vector_count), lambda j: (j, 0, 0)),
            pl.BlockSpec((2 * vector_count, 2 * vector_count), lambda j: (0, 0)),
        ],
        out_specs=pl.BlockSpec((1, 2, vector_count, vector_count), lambda j: (0, 0, 0, j)),
        name="finish",
    )(propagated, source_big)


def fits(mesh, eigenvectors, perambulator):
    space, slots = mesh.shape["space"], mesh.shape["tm"]
    vector_count = eigenvectors.shape[4]
    return (
        space == 4
        and slots == 4
        and eigenvectors.shape[0] == slots * mesh.shape["cfg"]
        and perambulator.shape[2] == space * vector_count
        and vector_count % 128 == 0
        and eigenvectors.shape[3] % (32 * space) == 0
    )


def solution(mesh):
    placed = (
        P(("cfg", "tm"), None, None, "space", None),
        P(("cfg", "tm"), None, None, "space"),
        P(),
        P(),
        P(),
    )

    def program(eigenvectors, perambulator, momenta, ratios, source_slice):
        chosen = body if fits(mesh, eigenvectors, perambulator) else general_body
        mapped = jax.shard_map(
            chosen,
            mesh=mesh,
            in_specs=placed,
            out_specs=P(("cfg", "tm"), None, "space", None),
            check_vma=False,
        )
        return mapped(eigenvectors, perambulator, momenta, ratios, source_slice)

    return program
```

profile of v0, /device:TPU:0, one launch (start us, length us, event | category | flops | bytes accessed | tf_op | source)
XLA Modules:
  0.0 80.7 jit_solution(14205302964780375026)
XLA Ops:
  0.7 74.0 %exchange.1 = (bf16[4,384,768]{2,1,0:T(8,128)(2,1)}, bf16[768,768]{1,0:T(8,128)(2,1)}) custom-call(s32[2,3]{1,0:T(2,128)} %momenta_ref.1, s32[2,2]{1,0:T(2,128)} %ratio_ref.1, s32[1]{0:T(128)S(6)} %copy.6.slice_ref, bf16[1,2,3,768,384]{4,3,2,1,0:T(8,128)(2,1)} %eig_hbm.1, bf16[1,2,1536,384]{3,2,1,0:T(8,128)(2,1)} %tau_hbm.1), custom_call_target="tpu_custom_call" | custom-call | tf_op jit(solution)/shard_map/exchange/pallas_call | solution.py:448
  74.7 6.0 %finish.1 = f32[1,2,384,1536]{3,2,1,0:T(8,128)} custom-call(bf16[4,384,768]{2,1,0:T(8,128)(2,1)} %get-tuple-element.7.prop_ref, bf16[768,768]{1,0:T(8,128)(2,1)} %get-tuple-element.8.source_ref), custom_call_target="tpu_custom_call" | custom-call | tf_op jit(solution)/shard_map/finish/pallas_call | solution.py:476
where the time goes:
time: 80.9 us; the launch traced here: 80.7 us
  Pallas kernels  80 us (99%)
    pallas_call x1, Pallas kernels, body(): pl.pallas_call(functools.partial(exchange_kernel, normalizer=normalizer),...  74 us
    pallas_call x1, Pallas kernels, body(): pl.pallas_call(finish_kernel, grid=(group,), out_shape=jax.ShapeDtypeStru...  6 us

commit v1 on v0

--- a/solution.py
+++ b/solution.py
@@ -11,6 +11,8 @@
 MESH = pl.DeviceIdType.MESH
 
 LSIDE = 64
+
+VMEM_BYTES = 67043328
 
 
 def spread(value, axis, source):
@@ -161,11 +163,11 @@
     slice_ref,
     eig_hbm,
     tau_hbm,
-    prop_ref,
-    source_ref,
+    res_ref,
     eig,
     acc,
     tau,
+    tau_mine,
     part,
     pair_out,
     pair_in,
@@ -176,20 +178,30 @@
     picked,
     far,
     sink_big,
+    source_big,
+    source_late,
+    prop,
+    prop_out,
+    prop_in,
     cosines,
     sines,
     eig_sem,
     own_sem,
     tau_send,
     tau_recv,
+    early_send,
+    early_recv,
     pair_send,
     pair_recv,
     cross_send,
     cross_recv,
     back_send,
     back_recv,
+    prop_send,
+    prop_recv,
     spread_send,
     spread_recv,
+    ready,
     *,
     normalizer,
 ):
@@ -198,6 +210,10 @@
     chunk_count, chunk_rows = part.shape[0], part.shape[2]
     step_count, site_step = eig.shape[0], eig.shape[2]
     steps_per_color = site_count // site_step
+    late_count = tau_mine.shape[2]
+    early_count = vector_count - late_count
+    piece_count = prop_send.shape[0]
+    piece_rows = vector_count // piece_count
     me = lax.axis_index("space")
     slot = lax.axis_index("tm")
     near = me + 1 - 2 * (me % 2)
@@ -217,25 +233,24 @@
     for step in range(step_count):
         eig_copy(step).start()
     own_copy = pltpu.make_async_copy(
-        tau_hbm.at[0, :, pl.ds(me * vector_count, vector_count), :], tau.at[me], own_sem
+        tau_hbm.at[0, :, pl.ds(me * vector_count, vector_count), :], tau.at[me], own_sem.at[0]
+    )
+    late_copy = pltpu.make_async_copy(
+        tau_hbm.at[
+            0, :, pl.ds(across * vector_count, vector_count), pl.ds(early_count, late_count)
+        ],
+        tau_mine,
+        own_sem.at[1],
     )
 
     barrier = pltpu.get_barrier_semaphore()
-    for peer in (near, across, mirror):
-        pl.semaphore_signal(barrier, inc=1, device_id={"space": peer}, device_id_type=MESH)
-    for peer in (core_peer, chip_peer):
-        pl.semaphore_signal(barrier, inc=1, device_id={"tm": peer}, device_id_type=MESH)
-    pl.semaphore_wait(barrier, 5)
-
-    def tau_copy(index, to, piece):
-        return pltpu.make_async_remote_copy(
-            src_ref=tau_hbm.at[0, piece, pl.ds(to * vector_count, vector_count), :],
-            dst_ref=tau.at[me, piece],
-            send_sem=tau_send.at[index, piece],
-            recv_sem=tau_recv.at[me, piece],
-            device_id={"space": to},
-            device_id_type=MESH,
-        )
+
+    def hello(peer):
+        pl.semaphore_signal(barrier, inc=1, device_id=peer, device_id_type=MESH)
+
+    hello({"space": near})
+    hello({"tm": core_peer})
+    hello({"tm": chip_peer})
 
     def hop(from_ref, to_ref, send_sem, recv_sem, peer):
         return pltpu.make_async_remote_copy(
@@ -247,18 +262,60 @@
             device_id_type=MESH,
         )
 
+    def tau_copy(index, to, piece):
+        return hop(
+            tau_hbm.at[0, piece, pl.ds(to * vector_count, vector_count), :],
+            tau.at[me, piece],
+            tau_send.at[index, piece],
+            tau_recv.at[me, piece],
+            {"space": to},
+        )
+
     near_copies = [tau_copy(0, near, piece) for piece in range(2)]
     across_copies = [tau_copy(1, across, piece) for piece in range(2)]
     mirror_copies = [tau_copy(2, mirror, piece) for piece in range(2)]
+    early_copy = hop(
+        tau_hbm.at[0, :, pl.ds(across * vector_count, vector_count), pl.ds(0, early_count)],
+        tau.at[me, :, :, pl.ds(0, early_count)],
+        early_send,
+        early_recv,
+        {"space": across},
+    )
+    prop_copies = [
+        hop(
+            prop_out.at[pl.ds(p * piece_rows, piece_rows), :],
+            prop_in.at[pl.ds(p * piece_rows, piece_rows), :],
+            prop_send.at[p],
+            prop_recv.at[p],
+            {"space": across},
+        )
+        for p in range(piece_count)
+    ]
+
+    def tell(index, peer):
+        pl.semaphore_signal(
+            ready.at[index], inc=1, device_id={"space": peer}, device_id_type=MESH
+        )
 
     @pl.when(inner == 1)
     def _():
+        hello({"space": mirror})
+        pl.semaphore_wait(barrier, 4)
         mirror_copies[0].start()
         mirror_copies[1].start()
-        across_copies[0].start()
-
-    near_copies[0].start()
-    near_copies[1].start()
+        near_copies[0].start()
+        near_copies[1].start()
+        tell(0, near)
+        tell(0, mirror)
+        pl.semaphore_wait(ready.at[0], 1)
+        tell(1, near)
+        late_copy.start()
+
+    @pl.when(inner == 0)
+    def _():
+        pl.semaphore_wait(barrier, 3)
+        near_copies[0].start()
+
     own_copy.start()
 
     lanes = cosines.shape[1]
@@ -339,14 +396,15 @@
             for c in range(2):
                 pair_out[q, c] = weighted(q, c).astype(jnp.bfloat16)
             pair_hops[q].start()
+        near_copies[1].start()
+        pl.semaphore_wait(ready.at[0], 1)
+        pl.semaphore_wait(ready.at[1], 1)
         for q in range(chunk_count // 2):
             back_hops[q].wait_recv()
         for copy in across_copies + mirror_copies:
             copy.start()
         for q in range(chunk_count // 2, chunk_count):
             back_hops[q].wait_recv()
-        for q in range(chunk_count):
-            pair_hops[q].wait_send()
 
     @pl.when(inner == 1)
     def _():
@@ -358,14 +416,11 @@
             part[q] = part[q] + pair_in[q].astype(jnp.float32)
             cross_out[q] = part[q].astype(jnp.bfloat16)
             cross_hops[q].start()
-        across_copies[1].start()
+        early_copy.start()
         for q in range(chunk_count):
             cross_hops[q].wait_recv()
             sink[q] = (part[q] + cross_in[q].astype(jnp.float32)).astype(jnp.bfloat16)
             back_hops[q].start()
-        for q in range(chunk_count):
-            cross_hops[q].wait_send()
-            back_hops[q].wait_send()
 
     core_hop = hop(sink, sink_pair, spread_send.at[0], spread_recv.at[0], {"tm": core_peer})
     core_hop.start()
@@ -377,20 +432,21 @@
         sink_big[rows, vector_count:] = -imag
         sink_big[low, :vector_count] = imag
         sink_big[low, vector_count:] = real
-    core_hop.wait()
-    chosen_slot = slice_ref[0] % lax.axis_size("tm")
-    picked[...] = jnp.where(chosen_slot == slot, sink[...], sink_pair[...])
-    half = pl.ds(core * (chunk_count // 2), chunk_count // 2)
-    chip_hop = hop(
-        picked.at[half], far.at[half], spread_send.at[1], spread_recv.at[1], {"tm": chip_peer}
-    )
-    chip_hop.start()
-
-    def carry_block(origin):
-        stacked = tau[origin].reshape(2 * vector_count, vector_count)
+
+    def carried(block):
+        stacked = block.reshape(2 * vector_count, block.shape[2])
         product = block_dot(sink_big[...], stacked, 1, 0).astype(jnp.bfloat16)
-        prop_ref[origin, :, :vector_count] = product[:vector_count]
-        prop_ref[origin, :, vector_count:] = product[vector_count:]
+        return product[:vector_count], product[vector_count:]
+
+    def left_multiply(origin):
+        real, imag = carried(tau[origin])
+        prop[origin, :, :vector_count] = real
+        prop[origin, :, vector_count:] = imag
+
+    def right_multiply(origin):
+        product = block_dot(prop[origin], source_big[...], 1, 1)
+        res_ref[origin, 0] = product[:, :vector_count]
+        res_ref[origin, 1] = product[:, vector_count:]
 
     def arrived(origin):
         for piece in range(2):
@@ -399,37 +455,115 @@
                 tau.at[origin, piece],
                 tau_send.at[0, piece],
                 tau_recv.at[origin, piece],
-                {"space": origin},
+                {"space": near},
             ).wait_recv()
 
+    @pl.when(inner == 1)
+    def _():
+        late_copy.wait()
+        real, imag = carried(tau_mine[...])
+        prop_out[:, :late_count] = real
+        prop_out[:, late_count:] = imag
+        for copy in prop_copies:
+            copy.start()
+
+    core_hop.wait()
+    chosen_slot = slice_ref[0] % lax.axis_size("tm")
+    picked[...] = jnp.where(chosen_slot == slot, sink[...], sink_pair[...])
+    half = pl.ds(core * (chunk_count // 2), chunk_count // 2)
+    chip_hop = hop(
+        picked.at[half], far.at[half], spread_send.at[1], spread_recv.at[1], {"tm": chip_peer}
+    )
+    chip_hop.start()
+
     own_copy.wait()
-    carry_block(me)
+    left_multiply(me)
     chip_hop.wait()
     forward_hop = hop(
         far.at[half], far.at[half], spread_send.at[2], spread_recv.at[2], {"tm": core_peer}
     )
     forward_hop.start()
+    arrived(near)
+    left_multiply(near)
     forward_hop.wait()
     chosen = jnp.where(chosen_slot // 2 == slot // 2, picked[...], far[...])
     for q in range(chunk_count):
         rows = pl.ds(q * chunk_rows, chunk_rows)
         low = pl.ds(vector_count + q * chunk_rows, chunk_rows)
-        source_ref[rows, :vector_count] = chosen[q, 0]
-        source_ref[rows, vector_count:] = chosen[q, 1]
-        source_ref[low, :vector_count] = -chosen[q, 1]
-        source_ref[low, vector_count:] = chosen[q, 0]
-    for origin in (near, across, mirror):
-        arrived(origin)
-        carry_block(origin)
-    for copy in near_copies + across_copies + mirror_copies:
+        source_big[rows, :vector_count] = chosen[q, 0]
+        source_big[rows, vector_count:] = chosen[q, 1]
+        source_big[low, :vector_count] = -chosen[q, 1]
+        source_big[low, vector_count:] = chosen[q, 0]
+    right_multiply(me)
+    right_multiply(near)
+
+    @pl.when(inner == 1)
+    def _():
+        for origin in (mirror, across):
+            arrived(origin)
+            left_multiply(origin)
+            right_multiply(origin)
+        for copy in mirror_copies + prop_copies:
+            copy.wait_send()
+        early_copy.wait_send()
+        for q in range(chunk_count):
+            cross_hops[q].wait_send()
+            back_hops[q].wait_send()
+
+    @pl.when(inner == 0)
+    def _():
+        early_copy.wait_recv()
+        real, imag = carried(tau[across, :, :, :early_count])
+        both = jnp.concatenate([real, imag], axis=1)
+        source_early = jnp.concatenate(
+            [
+                source_big[:, :early_count],
+                source_big[:, vector_count : vector_count + early_count],
+            ],
+            axis=1,
+        )
+        product = block_dot(both, source_early, 1, 1)
+        res_ref[across, 0] = product[:, :vector_count]
+        res_ref[across, 1] = product[:, vector_count:]
+        source_late[:, :late_count] = source_big[:, early_count:vector_count]
+        source_late[:, late_count:] = source_big[:, vector_count + early_count :]
+        arrived(mirror)
+        left_multiply(mirror)
+        right_multiply(mirror)
+        for q in range(chunk_count):
+            pair_hops[q].wait_send()
+        for copy in across_copies + mirror_copies:
+            copy.wait_send()
+        for p in range(piece_count):
+            rows = pl.ds(p * piece_rows, piece_rows)
+            prop_copies[p].wait_recv()
+            product = block_dot(prop_in[rows, :], source_late[...], 1, 1)
+            res_ref[across, 0, rows, :] += product[:, :vector_count]
+            res_ref[across, 1, rows, :] += product[:, vector_count:]
+
+    for copy in near_copies:
         copy.wait_send()
 
 
-def finish_kernel(prop_ref, source_ref, out_ref):
-    vector_count = source_ref.shape[0] // 2
-    product = block_dot(prop_ref[0], source_ref[...], 1, 1)
-    out_ref[0, 0] = product[:, :vector_count]
-    out_ref[0, 1] = product[:, vector_count:]
+def finish_kernel(res_ref, out_hbm, sems):
+    group, _, vector_count, _ = res_ref.shape
+    copies = [
+        pltpu.make_async_copy(
+            res_ref.at[origin, c],
+            out_hbm.at[0, c, :, pl.ds(origin * vector_count, vector_count)],
+            sems.at[origin, c],
+        )
+        for origin in range(group)
+        for c in range(2)
+    ]
+    for copy in copies:
+        copy.start()
+    for copy in copies:
+        copy.wait()
+
+
+def in_hbm(array):
+    return pltpu.with_memory_space_constraint(array, pltpu.HBM)
 
 
 def body(eigenvectors, perambulator, momenta, ratios, source_slice):
@@ -439,51 +573,70 @@
     site_step = site_count // 2
     step_count = 2 * color_count
     chunk_count = 4
+    piece_count = 4
+    late_count = vector_count - 128
     whole = (chunk_count, 2, vector_count // chunk_count, vector_count)
     bf16, f32 = jnp.bfloat16, jnp.float32
     smem = pl.BlockSpec(memory_space=pltpu.SMEM)
     vmem = pl.BlockSpec(memory_space=pltpu.VMEM)
     anywhere = pl.BlockSpec(memory_space=pl.ANY)
     dma = pltpu.SemaphoreType.DMA
-    propagated, source_big = pl.pallas_call(
+    room = 4 * group * 2 * vector_count * vector_count
+    result = pl.pallas_call(
         functools.partial(exchange_kernel, normalizer=normalizer),
-        out_shape=(
-            jax.ShapeDtypeStruct((group, vector_count, 2 * vector_count), bf16),
-            jax.ShapeDtypeStruct((2 * vector_count, 2 * vector_count), bf16),
-        ),
+        out_shape=pltpu.VMEM((group, 2, vector_count, vector_count), f32),
         in_specs=[smem, smem, smem, anywhere, anywhere],
-        out_specs=(vmem, vmem),
+        out_specs=vmem,
         scratch_shapes=[
             pltpu.VMEM((step_count, 2, site_step, vector_count), bf16),
             pltpu.VMEM((vector_count, 4 * vector_count), f32),
             pltpu.VMEM((group, 2, vector_count, vector_count), bf16),
+            pltpu.VMEM((2, vector_count, late_count), bf16),
             pltpu.VMEM(whole, f32),
             *[pltpu.VMEM(whole, bf16) for _ in range(8)],
             pltpu.VMEM((2 * vector_count, 2 * vector_count), bf16),
+            pltpu.VMEM((2 * vector_count, 2 * vector_count), bf16),
+            pltpu.VMEM((2 * vector_count, 2 * late_count), bf16),
+            pltpu.VMEM((group, vector_count, 2 * vector_count), bf16),
+            pltpu.VMEM((vector_count, 2 * late_count), bf16),
+            pltpu.VMEM((vector_count, 2 * late_count), bf16),
             pltpu.VMEM((site_count, 128), f32),
             pltpu.VMEM((site_count, 128), f32),
             dma((step_count,)),
-            dma,
+            dma((2,)),
             dma((3, 2)),
             dma((group, 2)),
+            dma,
+            dma,
             *[dma((chunk_count,)) for _ in range(6)],
+            dma((piece_count,)),
+            dma((piece_count,)),
             dma((3,)),
             dma((3,)),
+            pltpu.SemaphoreType.REGULAR((2,)),
         ],
-        compiler_params=pltpu.CompilerParams(collective_id=0, has_side_effects=True),
+        compiler_params=pltpu.CompilerParams(
+            collective_id=0,
+            has_side_effects=True,
+            vmem_limit_bytes=VMEM_BYTES - 3 * room,
+        ),
         name="exchange",
-    )(momenta, ratios, source_slice, eigenvectors, perambulator)
+    )(
+        in_hbm(momenta),
+        in_hbm(ratios),
+        source_slice,
+        in_hbm(eigenvectors),
+        in_hbm(perambulator),
+    )
     return pl.pallas_call(
         finish_kernel,
-        grid=(group,),
         out_shape=jax.ShapeDtypeStruct((1, 2, vector_count, group * vector_count), f32),
-        in_specs=[
-            pl.BlockSpec((1, vector_count, 2 * vector_count), lambda j: (j, 0, 0)),
-            pl.BlockSpec((2 * vector_count, 2 * vector_count), lambda j: (0, 0)),
-        ],
-        out_specs=pl.BlockSpec((1, 2, vector_count, vector_count), lambda j: (0, 0, 0, j)),
+        in_specs=[vmem],
+        out_specs=anywhere,
+        scratch_shapes=[dma((group, 2))],
+        compiler_params=pltpu.CompilerParams(vmem_limit_bytes=VMEM_BYTES // 2),
         name="finish",
-    )(propagated, source_big)
+    )(pltpu.with_memory_space_constraint(result, pltpu.VMEM))
 
 
 def fits(mesh, eigenvectors, perambulator):
@@ -495,6 +648,7 @@
         and eigenvectors.shape[0] == slots * mesh.shape["cfg"]
         and perambulator.shape[2] == space * vector_count
         and vector_count % 128 == 0
+        and vector_count > 128
         and eigenvectors.shape[3] % (32 * space) == 0
     )
 

time: 80.9 us -> 76.8 us (0.949)
  Pallas kernels: 80 us -> 76 us
    pallas_call x1, Pallas kernels: 6 us -> 2.24 us  [body(): pl.pallas_call(finish_kernel, out_shape=jax.ShapeDtypeStruct((1, 2, vecto...]
where the time goes in v1:
time: 76.8 us; the launch traced here: 76.7 us
  Pallas kernels  76 us (99%)
    pallas_call x1, Pallas kernels, body(): pl.pallas_call(functools.partial(exchange_kernel, normalizer=normalizer),...  73.8 us
    pallas_call x1, Pallas kernels, body(): pl.pallas_call(finish_kernel, out_shape=jax.ShapeDtypeStruct((1, 2, vecto...  2.24 us

profile of v1, /device:TPU:0, one launch (start us, length us, event | category | flops | bytes accessed | tf_op | source)
XLA Modules:
  0.0 76.7 jit_solution(297362415959863561)
XLA Ops:
  0.7 73.8 %exchange.1.res_ref = f32[4,2,384,384]{3,2,1,0:T(8,128)S(1)} custom-call(s32[2,3]{1,0:T(2,128)} %momenta_ref.1, s32[2,2]{1,0:T(2,128)} %ratio_ref.1, s32[1]{0:T(128)S(6)} %copy.6.slice_ref, bf16[1,2,3,768,384]{4,3,2,1,0:T(8,128)(2,1)} %eig_hbm.1, bf16[1,2,1536,384]{3,2,1,0:T(8,128)(2,1)} %tau_hbm.1), custom_call_target="tpu_custom_call" | custom-call | tf_op jit(solution)/shard_map/exchange/pallas_call | solution.py:585
  74.4 2.2 %finish.1 = f32[1,2,384,1536]{3,2,1,0:T(8,128)} custom-call(f32[4,2,384,384]{3,2,1,0:T(8,128)S(1)} %exchange.1.res_ref), custom_call_target="tpu_custom_call" | custom-call | tf_op jit(solution)/shard_map/finish/pallas_call | solution.py:631

commit v2 on v1

--- a/solution.py
+++ b/solution.py
@@ -158,12 +158,14 @@
 
 
 def exchange_kernel(
-    momenta_ref,
-    ratio_ref,
+    momenta_hbm,
+    ratio_hbm,
     slice_ref,
     eig_hbm,
     tau_hbm,
     res_ref,
+    momenta_ref,
+    ratio_ref,
     eig,
     acc,
     tau,
@@ -230,18 +232,20 @@
             eig_hbm.at[0, :, color, pl.ds(first, site_step), :], eig.at[step], eig_sem.at[step]
         )
 
-    for step in range(step_count):
-        eig_copy(step).start()
     own_copy = pltpu.make_async_copy(
         tau_hbm.at[0, :, pl.ds(me * vector_count, vector_count), :], tau.at[me], own_sem.at[0]
     )
     late_copy = pltpu.make_async_copy(
         tau_hbm.at[
-            0, :, pl.ds(across * vector_count, vector_count), pl.ds(early_count, late_count)
+            0, :, pl.ds(mirror * vector_count, vector_count), pl.ds(early_count, late_count)
         ],
         tau_mine,
         own_sem.at[1],
     )
+    scalar_copies = [
+        pltpu.make_async_copy(momenta_hbm, momenta_ref, own_sem.at[2]),
+        pltpu.make_async_copy(ratio_hbm, ratio_ref, own_sem.at[3]),
+    ]
 
     barrier = pltpu.get_barrier_semaphore()
 
@@ -251,6 +255,10 @@
     hello({"space": near})
     hello({"tm": core_peer})
     hello({"tm": chip_peer})
+    for copy in scalar_copies:
+        copy.start()
+    for step in range(step_count):
+        eig_copy(step).start()
 
     def hop(from_ref, to_ref, send_sem, recv_sem, peer):
         return pltpu.make_async_remote_copy(
@@ -274,65 +282,76 @@
     near_copies = [tau_copy(0, near, piece) for piece in range(2)]
     across_copies = [tau_copy(1, across, piece) for piece in range(2)]
     mirror_copies = [tau_copy(2, mirror, piece) for piece in range(2)]
-    early_copy = hop(
-        tau_hbm.at[0, :, pl.ds(across * vector_count, vector_count), pl.ds(0, early_count)],
-        tau.at[me, :, :, pl.ds(0, early_count)],
-        early_send,
-        early_recv,
-        {"space": across},
-    )
+    def early_copy(piece):
+        first, count = early_rows[piece]
+        return hop(
+            tau_hbm.at[
+                0, :, pl.ds(mirror * vector_count + first, count), pl.ds(0, early_count)
+            ],
+            tau.at[me, :, pl.ds(first, count), pl.ds(0, early_count)],
+            early_send.at[piece],
+            early_recv.at[piece],
+            {"space": mirror},
+        )
+
+    lead = vector_count // 3 // 32 * 32
+    early_rows = [(0, lead), (lead, vector_count - lead)]
+    early_copies = [early_copy(piece) for piece in range(2)]
     prop_copies = [
         hop(
             prop_out.at[pl.ds(p * piece_rows, piece_rows), :],
             prop_in.at[pl.ds(p * piece_rows, piece_rows), :],
             prop_send.at[p],
             prop_recv.at[p],
-            {"space": across},
+            {"space": mirror},
         )
         for p in range(piece_count)
     ]
 
     def tell(index, peer):
-        pl.semaphore_signal(
-            ready.at[index], inc=1, device_id={"space": peer}, device_id_type=MESH
-        )
+        pl.semaphore_signal(ready.at[index], inc=1, device_id=peer, device_id_type=MESH)
+
+    def phases():
+        for copy in scalar_copies:
+            copy.wait()
+        lanes = cosines.shape[1]
+        site = me * site_count + lax.broadcasted_iota(jnp.int32, (site_count, lanes), 0)
+        first_lane = lax.broadcasted_iota(jnp.int32, (site_count, lanes), 1) == 0
+        shift = LSIDE.bit_length() - 1
+        places = (
+            jnp.bitwise_and(site, LSIDE - 1),
+            jnp.bitwise_and(jnp.right_shift(site, shift), LSIDE - 1),
+            jnp.right_shift(site, 2 * shift),
+        )
+        turn = jnp.zeros_like(site)
+        for axis in range(3):
+            turn += jnp.where(first_lane, momenta_ref[0, axis], momenta_ref[1, axis]) * places[axis]
+        angle = jnp.bitwise_and(turn, LSIDE - 1).astype(jnp.float32) * (2.0 * math.pi / LSIDE)
+        cosines[...] = jnp.cos(angle)
+        sines[...] = jnp.sin(angle)
 
     @pl.when(inner == 1)
     def _():
         hello({"space": mirror})
         pl.semaphore_wait(barrier, 4)
-        mirror_copies[0].start()
-        mirror_copies[1].start()
+        tell(0, {"space": mirror})
+        early_copies[0].start()
+        tell(0, {"space": near})
         near_copies[0].start()
-        near_copies[1].start()
-        tell(0, near)
-        tell(0, mirror)
+        phases()
         pl.semaphore_wait(ready.at[0], 1)
-        tell(1, near)
+        for copy in across_copies:
+            copy.start()
+        tell(1, {"space": near})
         late_copy.start()
 
     @pl.when(inner == 0)
     def _():
+        phases()
         pl.semaphore_wait(barrier, 3)
         near_copies[0].start()
 
     own_copy.start()
-
-    lanes = cosines.shape[1]
-    site = me * site_count + lax.broadcasted_iota(jnp.int32, (site_count, lanes), 0)
-    first_lane = lax.broadcasted_iota(jnp.int32, (site_count, lanes), 1) == 0
-    shift = LSIDE.bit_length() - 1
-    places = (
-        jnp.bitwise_and(site, LSIDE - 1),
-        jnp.bitwise_and(jnp.right_shift(site, shift), LSIDE - 1),
-        jnp.right_shift(site, 2 * shift),
-    )
-    turn = jnp.zeros_like(site)
-    for axis in range(3):
-        turn += jnp.where(first_lane, momenta_ref[0, axis], momenta_ref[1, axis]) * places[axis]
-    angle = jnp.bitwise_and(turn, LSIDE - 1).astype(jnp.float32) * (2.0 * math.pi / LSIDE)
-    cosines[...] = jnp.cos(angle)
-    sines[...] = jnp.sin(angle)
 
     acc[...] = jnp.zeros_like(acc)
 
@@ -399,28 +418,39 @@
         near_copies[1].start()
         pl.semaphore_wait(ready.at[0], 1)
         pl.semaphore_wait(ready.at[1], 1)
-        for q in range(chunk_count // 2):
+        for q in range(chunk_count - 1):
             back_hops[q].wait_recv()
+        tell(2, {"tm": core_peer})
+        pl.semaphore_wait(ready.at[2], 1)
         for copy in across_copies + mirror_copies:
             copy.start()
-        for q in range(chunk_count // 2, chunk_count):
-            back_hops[q].wait_recv()
+        back_hops[chunk_count - 1].wait_recv()
 
     @pl.when(inner == 1)
     def _():
         for q in range(chunk_count):
             for c in range(2):
                 part[q, c] = weighted(q, c)
-        for q in range(chunk_count):
+
+        def forward(q):
             pair_hops[q].wait_recv()
             part[q] = part[q] + pair_in[q].astype(jnp.float32)
             cross_out[q] = part[q].astype(jnp.bfloat16)
             cross_hops[q].start()
-        early_copy.start()
-        for q in range(chunk_count):
+
+        def settle(q):
             cross_hops[q].wait_recv()
             sink[q] = (part[q] + cross_in[q].astype(jnp.float32)).astype(jnp.bfloat16)
             back_hops[q].start()
+
+        for q in range(chunk_count):
+            forward(q)
+            if q == chunk_count - 1:
+                early_copies[1].start()
+            if q > 0:
+                settle(q - 1)
+        settle(chunk_count - 1)
+        near_copies[1].start()
 
     core_hop = hop(sink, sink_pair, spread_send.at[0], spread_recv.at[0], {"tm": core_peer})
     core_hop.start()
@@ -478,13 +508,22 @@
 
     own_copy.wait()
     left_multiply(me)
+
+    @pl.when(inner == 1)
+    def _():
+        arrived(near)
+        left_multiply(near)
+
+    @pl.when(inner == 0)
+    def _():
+        arrived(across)
+        left_multiply(across)
+
     chip_hop.wait()
     forward_hop = hop(
         far.at[half], far.at[half], spread_send.at[2], spread_recv.at[2], {"tm": core_peer}
     )
     forward_hop.start()
-    arrived(near)
-    left_multiply(near)
     forward_hop.wait()
     chosen = jnp.where(chosen_slot // 2 == slot // 2, picked[...], far[...])
     for q in range(chunk_count):
@@ -495,26 +534,33 @@
         source_big[low, :vector_count] = -chosen[q, 1]
         source_big[low, vector_count:] = chosen[q, 0]
     right_multiply(me)
-    right_multiply(near)
-
-    @pl.when(inner == 1)
-    def _():
-        for origin in (mirror, across):
+
+    @pl.when(inner == 0)
+    def _():
+        right_multiply(across)
+        for origin in (near, mirror):
             arrived(origin)
             left_multiply(origin)
             right_multiply(origin)
-        for copy in mirror_copies + prop_copies:
+        for q in range(chunk_count):
+            pair_hops[q].wait_send()
+        for copy in across_copies + mirror_copies:
             copy.wait_send()
-        early_copy.wait_send()
+
+    @pl.when(inner == 1)
+    def _():
+        right_multiply(near)
         for q in range(chunk_count):
             cross_hops[q].wait_send()
             back_hops[q].wait_send()
-
-    @pl.when(inner == 0)
-    def _():
-        early_copy.wait_recv()
-        real, imag = carried(tau[across, :, :, :early_count])
-        both = jnp.concatenate([real, imag], axis=1)
+        for copy in across_copies:
+            copy.wait_send()
+        arrived(across)
+        left_multiply(across)
+        right_multiply(across)
+        for copy in early_copies:
+            copy.wait_recv()
+        both = jnp.concatenate(carried(tau[mirror, :, :, :early_count]), axis=1)
         source_early = jnp.concatenate(
             [
                 source_big[:, :early_count],
@@ -523,23 +569,20 @@
             axis=1,
         )
         product = block_dot(both, source_early, 1, 1)
-        res_ref[across, 0] = product[:, :vector_count]
-        res_ref[across, 1] = product[:, vector_count:]
+        res_ref[mirror, 0] = product[:, :vector_count]
+        res_ref[mirror, 1] = product[:, vector_count:]
         source_late[:, :late_count] = source_big[:, early_count:vector_count]
         source_late[:, late_count:] = source_big[:, vector_count + early_count :]
-        arrived(mirror)
-        left_multiply(mirror)
-        right_multiply(mirror)
-        for q in range(chunk_count):
-            pair_hops[q].wait_send()
-        for copy in across_copies + mirror_copies:
+        for copy in early_copies:
             copy.wait_send()
         for p in range(piece_count):
             rows = pl.ds(p * piece_rows, piece_rows)
             prop_copies[p].wait_recv()
             product = block_dot(prop_in[rows, :], source_late[...], 1, 1)
-            res_ref[across, 0, rows, :] += product[:, :vector_count]
-            res_ref[across, 1, rows, :] += product[:, vector_count:]
+            res_ref[mirror, 0, rows, :] += product[:, :vector_count]
+            res_ref[mirror, 1, rows, :] += product[:, vector_count:]
+        for copy in prop_copies:
+            copy.wait_send()
 
     for copy in near_copies:
         copy.wait_send()
@@ -574,7 +617,7 @@
     step_count = 2 * color_count
     chunk_count = 4
     piece_count = 4
-    late_count = vector_count - 128
+    late_count = 128
     whole = (chunk_count, 2, vector_count // chunk_count, vector_count)
     bf16, f32 = jnp.bfloat16, jnp.float32
     smem = pl.BlockSpec(memory_space=pltpu.SMEM)
@@ -585,9 +628,11 @@
     result = pl.pallas_call(
         functools.partial(exchange_kernel, normalizer=normalizer),
         out_shape=pltpu.VMEM((group, 2, vector_count, vector_count), f32),
-        in_specs=[smem, smem, smem, anywhere, anywhere],
+        in_specs=[anywhere, anywhere, smem, anywhere, anywhere],
         out_specs=vmem,
         scratch_shapes=[
+            pltpu.SMEM(momenta.shape, jnp.int32),
+            pltpu.SMEM(ratios.shape, jnp.int32),
             pltpu.VMEM((step_count, 2, site_step, vector_count), bf16),
             pltpu.VMEM((vector_count, 4 * vector_count), f32),
             pltpu.VMEM((group, 2, vector_count, vector_count), bf16),
@@ -603,17 +648,17 @@
             pltpu.VMEM((site_count, 128), f32),
             pltpu.VMEM((site_count, 128), f32),
             dma((step_count,)),
-            dma((2,)),
+            dma((4,)),
             dma((3, 2)),
             dma((group, 2)),
-            dma,
-            dma,
+            dma((2,)),
+            dma((2,)),
             *[dma((chunk_count,)) for _ in range(6)],
             dma((piece_count,)),
             dma((piece_count,)),
             dma((3,)),
             dma((3,)),
-            pltpu.SemaphoreType.REGULAR((2,)),
+            pltpu.SemaphoreType.REGULAR((3,)),
         ],
         compiler_params=pltpu.CompilerParams(
             collective_id=0,

time: 76.8 us -> 71.3 us (0.928)
  the two profiles are of different devices: /device:TPU:0 before, /device:TPU:8 now
where the time goes in v2:
time: 71.3 us; the launch traced here: 71.1 us
  Pallas kernels  70.3 us (99%)
  between operations  0.82 us (1%)
    pallas_call x1, Pallas kernels, body(): pl.pallas_call(functools.partial(exchange_kernel, normalizer=normalizer),...  68 us
    pallas_call x1, Pallas kernels, body(): pl.pallas_call(finish_kernel, out_shape=jax.ShapeDtypeStruct((1, 2, vecto...  2.24 us

profile of v2, /device:TPU:8, one launch (start us, length us, event | category | flops | bytes accessed | tf_op | source)
XLA Modules:
  0.0 71.1 jit_solution(5287014895599522038)
XLA Ops:
  0.7 68.0 %exchange.1.res_ref = f32[4,2,384,384]{3,2,1,0:T(8,128)S(1)} custom-call(s32[2,3]{1,0:T(2,128)} %momenta_hbm.1, s32[2,2]{1,0:T(2,128)} %ratio_hbm.1, s32[1]{0:T(128)S(6)} %copy.6.slice_ref, bf16[1,2,3,768,384]{4,3,2,1,0:T(8,128)(2,1)} %eig_hbm.1, bf16[1,2,1536,384]{3,2,1,0:T(8,128)(2,1)} %tau_hbm.1), custom_call_target="tpu_custom_call" | custom-call | tf_op jit(solution)/shard_map/exchange/pallas_call | solution.py:628
  68.7 2.2 %finish.1 = f32[1,2,384,1536]{3,2,1,0:T(8,128)} custom-call(f32[4,2,384,384]{3,2,1,0:T(8,128)S(1)} %exchange.1.res_ref), custom_call_target="tpu_custom_call" | custom-call | tf_op jit(solution)/shard_map/finish/pallas_call | solution.py:676

commit v3 on v2

--- a/solution.py
+++ b/solution.py
@@ -187,21 +187,9 @@
     prop_in,
     cosines,
     sines,
-    eig_sem,
     own_sem,
-    tau_send,
-    tau_recv,
-    early_send,
-    early_recv,
-    pair_send,
-    pair_recv,
-    cross_send,
-    cross_recv,
-    back_send,
-    back_recv,
-    prop_send,
-    prop_recv,
-    spread_send,
+    send,
+    recv,
     spread_recv,
     ready,
     *,
@@ -210,11 +198,13 @@
     vector_count = eig_hbm.shape[4]
     site_count = eig_hbm.shape[3]
     chunk_count, chunk_rows = part.shape[0], part.shape[2]
-    step_count, site_step = eig.shape[0], eig.shape[2]
+    color_count = eig.shape[1]
+    site_step = site_count // 2
     steps_per_color = site_count // site_step
+    step_count = color_count * steps_per_color
     late_count = tau_mine.shape[2]
     early_count = vector_count - late_count
-    piece_count = prop_send.shape[0]
+    piece_count = 4
     piece_rows = vector_count // piece_count
     me = lax.axis_index("space")
     slot = lax.axis_index("tm")
@@ -226,12 +216,7 @@
     core_peer = slot + 1 - 2 * core
     chip_peer = slot + 2 - 4 * (slot // 2)
 
-    def eig_copy(step):
-        color, first = step // steps_per_color, (step % steps_per_color) * site_step
-        return pltpu.make_async_copy(
-            eig_hbm.at[0, :, color, pl.ds(first, site_step), :], eig.at[step], eig_sem.at[step]
-        )
-
+    eig_copy = pltpu.make_async_copy(eig_hbm.at[0], eig, own_sem.at[4])
     own_copy = pltpu.make_async_copy(
         tau_hbm.at[0, :, pl.ds(me * vector_count, vector_count), :], tau.at[me], own_sem.at[0]
     )
@@ -251,14 +236,6 @@
 
     def hello(peer):
         pl.semaphore_signal(barrier, inc=1, device_id=peer, device_id_type=MESH)
-
-    hello({"space": near})
-    hello({"tm": core_peer})
-    hello({"tm": chip_peer})
-    for copy in scalar_copies:
-        copy.start()
-    for step in range(step_count):
-        eig_copy(step).start()
 
     def hop(from_ref, to_ref, send_sem, recv_sem, peer):
         return pltpu.make_async_remote_copy(
@@ -270,18 +247,19 @@
             device_id_type=MESH,
         )
 
-    def tau_copy(index, to, piece):
+    def tau_copy(to, part_of, recv_index):
         return hop(
-            tau_hbm.at[0, piece, pl.ds(to * vector_count, vector_count), :],
-            tau.at[me, piece],
-            tau_send.at[index, piece],
-            tau_recv.at[me, piece],
+            tau_hbm.at[0, part_of, pl.ds(to * vector_count, vector_count), :],
+            tau.at[me, part_of],
+            send.at[0],
+            recv.at[recv_index],
             {"space": to},
         )
 
-    near_copies = [tau_copy(0, near, piece) for piece in range(2)]
-    across_copies = [tau_copy(1, across, piece) for piece in range(2)]
-    mirror_copies = [tau_copy(2, mirror, piece) for piece in range(2)]
+    near_copies = [tau_copy(near, piece, piece) for piece in range(2)]
+    across_raw = tau_copy(across, slice(None), 6)
+    across_copies = [tau_copy(across, piece, 12 + piece) for piece in range(2)]
+    mirror_copy = tau_copy(mirror, slice(None), 7)
     def early_copy(piece):
         first, count = early_rows[piece]
         return hop(
@@ -289,20 +267,20 @@
                 0, :, pl.ds(mirror * vector_count + first, count), pl.ds(0, early_count)
             ],
             tau.at[me, :, pl.ds(first, count), pl.ds(0, early_count)],
-            early_send.at[piece],
-            early_recv.at[piece],
+            send.at[1],
+            recv.at[10 + piece],
             {"space": mirror},
         )
 
-    lead = vector_count // 3 // 32 * 32
+    lead = vector_count * 5 // 12 // 32 * 32
     early_rows = [(0, lead), (lead, vector_count - lead)]
     early_copies = [early_copy(piece) for piece in range(2)]
     prop_copies = [
         hop(
             prop_out.at[pl.ds(p * piece_rows, piece_rows), :],
             prop_in.at[pl.ds(p * piece_rows, piece_rows), :],
-            prop_send.at[p],
-            prop_recv.at[p],
+            send.at[1],
+            recv.at[14 + p],
             {"space": mirror},
         )
         for p in range(piece_count)
@@ -333,32 +311,48 @@
     @pl.when(inner == 1)
     def _():
         hello({"space": mirror})
-        pl.semaphore_wait(barrier, 4)
-        tell(0, {"space": mirror})
+        hello({"space": near})
+        pl.semaphore_wait(barrier, 1)
         early_copies[0].start()
+        for copy in scalar_copies:
+            copy.start()
+        eig_copy.start()
+        phases()
+        pl.semaphore_wait(ready.at[0], 1)
+        tell(1, {"space": mirror})
+        near_copies[0].start()
+        pl.semaphore_wait(ready.at[1], 1)
+        across_raw.start()
+        tell(2, {"space": near})
+        late_copy.start()
+
+    @pl.when(inner == 0)
+    def _():
+        hello({"tm": core_peer})
+        hello({"tm": chip_peer})
+        for copy in scalar_copies:
+            copy.start()
+        eig_copy.start()
+        pl.semaphore_wait(barrier, 3)
         tell(0, {"space": near})
         near_copies[0].start()
+        tell(0, {"tm": core_peer})
+        tell(1, {"tm": chip_peer})
         phases()
         pl.semaphore_wait(ready.at[0], 1)
-        for copy in across_copies:
-            copy.start()
-        tell(1, {"space": near})
-        late_copy.start()
-
-    @pl.when(inner == 0)
-    def _():
-        phases()
-        pl.semaphore_wait(barrier, 3)
-        near_copies[0].start()
+        pl.semaphore_wait(ready.at[1], 1)
+        tell(3, {"space": near})
 
     own_copy.start()
 
     acc[...] = jnp.zeros_like(acc)
 
+    eig_copy.wait()
+
     def accumulate(step, carry):
-        eig_copy(step).wait()
+        color = step // steps_per_color
         rows = pl.ds(pl.multiple_of((step % steps_per_color) * site_step, site_step), site_step)
-        plain_real, plain_imag = eig[step, 0], eig[step, 1]
+        plain_real, plain_imag = eig[0, color, rows, :], eig[1, color, rows, :]
         real = plain_real.astype(jnp.float32)
         imag = plain_imag.astype(jnp.float32)
         upper, lower = [], []
@@ -376,7 +370,7 @@
         acc[...] += block_dot(left, right, 0, 0)
         return carry
 
-    lax.fori_loop(0, step_count, accumulate, 0)
+    lax.fori_loop(0, step_count, accumulate, 0, unroll=True)
 
     weights = [
         jnp.full((1, vector_count), ratio_ref[k, 0], jnp.int32).astype(jnp.float32)
@@ -394,18 +388,18 @@
 
     pair_hops = [
         hop(
-            pair_out.at[q], pair_in.at[q], pair_send.at[q], pair_recv.at[q], {"space": near}
+            pair_out.at[q], pair_in.at[q], send.at[0], recv.at[2 + q], {"space": near}
         )
         for q in range(chunk_count)
     ]
     cross_hops = [
         hop(
-            cross_out.at[q], cross_in.at[q], cross_send.at[q], cross_recv.at[q], {"space": mirror}
+            cross_out.at[q], cross_in.at[q], send.at[0], recv.at[6 + q], {"space": mirror}
         )
         for q in range(chunk_count)
     ]
     back_hops = [
-        hop(sink.at[q], sink.at[q], back_send.at[q], back_recv.at[q], {"space": near})
+        hop(sink.at[q], sink.at[q], send.at[0], recv.at[2 + q], {"space": near})
         for q in range(chunk_count)
     ]
 
@@ -416,15 +410,16 @@
                 pair_out[q, c] = weighted(q, c).astype(jnp.bfloat16)
             pair_hops[q].start()
         near_copies[1].start()
-        pl.semaphore_wait(ready.at[0], 1)
-        pl.semaphore_wait(ready.at[1], 1)
-        for q in range(chunk_count - 1):
+        pl.semaphore_wait(ready.at[2], 1)
+        for q in range(chunk_count // 2):
             back_hops[q].wait_recv()
-        tell(2, {"tm": core_peer})
-        pl.semaphore_wait(ready.at[2], 1)
-        for copy in across_copies + mirror_copies:
-            copy.start()
-        back_hops[chunk_count - 1].wait_recv()
+        tell(4, {"tm": core_peer})
+        pl.semaphore_wait(ready.at[4], 1)
+        across_copies[0].start()
+        mirror_copy.start()
+        across_copies[1].start()
+        for q in range(chunk_count // 2, chunk_count):
+            back_hops[q].wait_recv()
 
     @pl.when(inner == 1)
     def _():
@@ -447,12 +442,14 @@
             forward(q)
             if q == chunk_count - 1:
                 early_copies[1].start()
-            if q > 0:
-                settle(q - 1)
-        settle(chunk_count - 1)
+            if q > 1:
+                settle(q - 2)
+        for q in range(chunk_count - 2, chunk_count):
+            settle(q)
         near_copies[1].start()
-
-    core_hop = hop(sink, sink_pair, spread_send.at[0], spread_recv.at[0], {"tm": core_peer})
+        pl.semaphore_wait(ready.at[3], 1)
+
+    core_hop = hop(sink, sink_pair, send.at[2], spread_recv.at[0], {"tm": core_peer})
     core_hop.start()
     for q in range(chunk_count):
         rows = pl.ds(q * chunk_rows, chunk_rows)
@@ -478,15 +475,9 @@
         res_ref[origin, 0] = product[:, :vector_count]
         res_ref[origin, 1] = product[:, vector_count:]
 
-    def arrived(origin):
-        for piece in range(2):
-            hop(
-                tau.at[origin, piece],
-                tau.at[origin, piece],
-                tau_send.at[0, piece],
-                tau_recv.at[origin, piece],
-                {"space": near},
-            ).wait_recv()
+    def arrived(copies):
+        for copy in copies:
+            copy.wait_recv()
 
     @pl.when(inner == 1)
     def _():
@@ -497,12 +488,12 @@
         for copy in prop_copies:
             copy.start()
 
-    core_hop.wait()
+    core_hop.wait_recv()
     chosen_slot = slice_ref[0] % lax.axis_size("tm")
     picked[...] = jnp.where(chosen_slot == slot, sink[...], sink_pair[...])
     half = pl.ds(core * (chunk_count // 2), chunk_count // 2)
     chip_hop = hop(
-        picked.at[half], far.at[half], spread_send.at[1], spread_recv.at[1], {"tm": chip_peer}
+        picked.at[half], far.at[half], send.at[2], spread_recv.at[1], {"tm": chip_peer}
     )
     chip_hop.start()
 
@@ -511,20 +502,20 @@
 
     @pl.when(inner == 1)
     def _():
-        arrived(near)
+        arrived(near_copies)
         left_multiply(near)
 
     @pl.when(inner == 0)
     def _():
-        arrived(across)
+        arrived([across_raw])
         left_multiply(across)
 
-    chip_hop.wait()
+    chip_hop.wait_recv()
     forward_hop = hop(
-        far.at[half], far.at[half], spread_send.at[2], spread_recv.at[2], {"tm": core_peer}
+        far.at[half], far.at[half], send.at[2], spread_recv.at[2], {"tm": core_peer}
     )
     forward_hop.start()
-    forward_hop.wait()
+    forward_hop.wait_recv()
     chosen = jnp.where(chosen_slot // 2 == slot // 2, picked[...], far[...])
     for q in range(chunk_count):
         rows = pl.ds(q * chunk_rows, chunk_rows)
@@ -538,28 +529,18 @@
     @pl.when(inner == 0)
     def _():
         right_multiply(across)
-        for origin in (near, mirror):
-            arrived(origin)
+        for origin, copies in ((near, near_copies), (mirror, [mirror_copy])):
+            arrived(copies)
             left_multiply(origin)
             right_multiply(origin)
-        for q in range(chunk_count):
-            pair_hops[q].wait_send()
-        for copy in across_copies + mirror_copies:
-            copy.wait_send()
 
     @pl.when(inner == 1)
     def _():
         right_multiply(near)
-        for q in range(chunk_count):
-            cross_hops[q].wait_send()
-            back_hops[q].wait_send()
-        for copy in across_copies:
-            copy.wait_send()
-        arrived(across)
+        arrived(across_copies)
         left_multiply(across)
         right_multiply(across)
-        for copy in early_copies:
-            copy.wait_recv()
+        arrived(early_copies)
         both = jnp.concatenate(carried(tau[mirror, :, :, :early_count]), axis=1)
         source_early = jnp.concatenate(
             [
@@ -571,38 +552,34 @@
         product = block_dot(both, source_early, 1, 1)
         res_ref[mirror, 0] = product[:, :vector_count]
         res_ref[mirror, 1] = product[:, vector_count:]
-        source_late[:, :late_count] = source_big[:, early_count:vector_count]
-        source_late[:, late_count:] = source_big[:, vector_count + early_count :]
-        for copy in early_copies:
-            copy.wait_send()
-        for p in range(piece_count):
+        source_late[:late_count] = source_big[:, early_count:vector_count].T
+        source_late[late_count:] = source_big[:, vector_count + early_count :].T
+
+        def add_piece(p):
             rows = pl.ds(p * piece_rows, piece_rows)
             prop_copies[p].wait_recv()
-            product = block_dot(prop_in[rows, :], source_late[...], 1, 1)
+            product = block_dot(prop_in[rows, :], source_late[...], 1, 0)
             res_ref[mirror, 0, rows, :] += product[:, :vector_count]
             res_ref[mirror, 1, rows, :] += product[:, vector_count:]
-        for copy in prop_copies:
-            copy.wait_send()
-
-    for copy in near_copies:
-        copy.wait_send()
-
-
-def finish_kernel(res_ref, out_hbm, sems):
+
+        for p in range(piece_count):
+            add_piece(p)
+        hop(sink, sink, send.at[1], recv.at[0], {"space": near}).wait_send()
+
+    hop(tau, tau, send.at[0], recv.at[0], {"space": near}).wait_send()
+    pair = pl.ds(0, 2)
+    hop(tau.at[pair], tau.at[pair], send.at[2], recv.at[0], {"space": near}).wait_send()
+
+
+def finish_kernel(res_ref, out_hbm, sem):
     group, _, vector_count, _ = res_ref.shape
-    copies = [
+    for origin in range(group):
         pltpu.make_async_copy(
-            res_ref.at[origin, c],
-            out_hbm.at[0, c, :, pl.ds(origin * vector_count, vector_count)],
-            sems.at[origin, c],
-        )
-        for origin in range(group)
-        for c in range(2)
-    ]
-    for copy in copies:
-        copy.start()
-    for copy in copies:
-        copy.wait()
+            res_ref.at[origin],
+            out_hbm.at[0, :, :, pl.ds(origin * vector_count, vector_count)],
+            sem,
+        ).start()
+    pltpu.make_async_copy(res_ref, res_ref, sem).wait()
 
 
 def in_hbm(array):
@@ -613,10 +590,7 @@
     color_count, site_count, vector_count = eigenvectors.shape[2:]
     group = lax.axis_size("space")
     normalizer = 1.0 / math.sqrt(color_count * site_count * group * vector_count)
-    site_step = site_count // 2
-    step_count = 2 * color_count
     chunk_count = 4
-    piece_count = 4
     late_count = 128
     whole = (chunk_count, 2, vector_count // chunk_count, vector_count)
     bf16, f32 = jnp.bfloat16, jnp.float32
@@ -633,7 +607,7 @@
         scratch_shapes=[
             pltpu.SMEM(momenta.shape, jnp.int32),
             pltpu.SMEM(ratios.shape, jnp.int32),
-            pltpu.VMEM((step_count, 2, site_step, vector_count), bf16),
+            pltpu.VMEM(eigenvectors.shape[1:], bf16),
             pltpu.VMEM((vector_count, 4 * vector_count), f32),
             pltpu.VMEM((group, 2, vector_count, vector_count), bf16),
             pltpu.VMEM((2, vector_count, late_count), bf16),
@@ -641,24 +615,17 @@
             *[pltpu.VMEM(whole, bf16) for _ in range(8)],
             pltpu.VMEM((2 * vector_count, 2 * vector_count), bf16),
             pltpu.VMEM((2 * vector_count, 2 * vector_count), bf16),
-            pltpu.VMEM((2 * vector_count, 2 * late_count), bf16),
+            pltpu.VMEM((2 * late_count, 2 * vector_count), bf16),
             pltpu.VMEM((group, vector_count, 2 * vector_count), bf16),
             pltpu.VMEM((vector_count, 2 * late_count), bf16),
             pltpu.VMEM((vector_count, 2 * late_count), bf16),
             pltpu.VMEM((site_count, 128), f32),
             pltpu.VMEM((site_count, 128), f32),
-            dma((step_count,)),
-            dma((4,)),
-            dma((3, 2)),
-            dma((group, 2)),
-            dma((2,)),
-            dma((2,)),
-            *[dma((chunk_count,)) for _ in range(6)],
-            dma((piece_count,)),
-            dma((piece_count,)),
+            dma((5,)),
             dma((3,)),
+            dma((18,)),
             dma((3,)),
-            pltpu.SemaphoreType.REGULAR((3,)),
+            pltpu.SemaphoreType.REGULAR((5,)),
         ],
         compiler_params=pltpu.CompilerParams(
             collective_id=0,
@@ -678,7 +645,7 @@
         out_shape=jax.ShapeDtypeStruct((1, 2, vector_count, group * vector_count), f32),
         in_specs=[vmem],
         out_specs=anywhere,
-        scratch_shapes=[dma((group, 2))],
+        scratch_shapes=[dma],
         compiler_params=pltpu.CompilerParams(vmem_limit_bytes=VMEM_BYTES // 2),
         name="finish",
     )(pltpu.with_memory_space_constraint(result, pltpu.VMEM))

time: 71.3 us -> 69.8 us (0.979)
  Pallas kernels: 70.3 us -> 68.8 us
    pallas_call x1, Pallas kernels: 68 us -> 66.6 us  [body(): pl.pallas_call(functools.partial(exchange_kernel, normalizer=normalizer),...]
where the time goes in v3:
time: 69.8 us; the launch traced here: 69.6 us
  Pallas kernels  68.8 us (99%)
  between operations  0.82 us (1%)
    pallas_call x1, Pallas kernels, body(): pl.pallas_call(functools.partial(exchange_kernel, normalizer=normalizer),...  66.6 us
    pallas_call x1, Pallas kernels, body(): pl.pallas_call(finish_kernel, out_shape=jax.ShapeDtypeStruct((1, 2, vecto...  2.19 us

profile of v3, /device:TPU:8, one launch (start us, length us, event | category | flops | bytes accessed | tf_op | source)
XLA Modules:
  0.0 69.6 jit_solution(16819997536148996045)
XLA Ops:
  0.7 66.6 %exchange.1.res_ref = f32[4,2,384,384]{3,2,1,0:T(8,128)S(1)} custom-call(s32[2,3]{1,0:T(2,128)} %momenta_hbm.1, s32[2,2]{1,0:T(2,128)} %ratio_hbm.1, s32[1]{0:T(128)S(6)} %copy.6.slice_ref, bf16[1,2,3,768,384]{4,3,2,1,0:T(8,128)(2,1)} %eig_hbm.1, bf16[1,2,1536,384]{3,2,1,0:T(8,128)(2,1)} %tau_hbm.1), custom_call_target="tpu_custom_call" | custom-call | tf_op jit(solution)/shard_map/exchange/pallas_call | solution.py:602
  67.3 2.2 %finish.1 = f32[1,2,384,1536]{3,2,1,0:T(8,128)} custom-call(f32[4,2,384,384]{3,2,1,0:T(8,128)S(1)} %exchange.1.res_ref), custom_call_target="tpu_custom_call" | custom-call | tf_op jit(solution)/shard_map/finish/pallas_call | solution.py:643

commit v4 on v3

--- a/solution.py
+++ b/solution.py
@@ -204,8 +204,11 @@
     step_count = color_count * steps_per_color
     late_count = tau_mine.shape[2]
     early_count = vector_count - late_count
-    piece_count = 4
-    piece_rows = vector_count // piece_count
+    last_rows = vector_count // 12 // 32 * 32
+    piece_rows = (vector_count - last_rows) // 3 // 32 * 32
+    piece_ends = [piece_rows, 2 * piece_rows, vector_count - last_rows, vector_count]
+    pieces = [pl.ds(a, b - a) for a, b in zip([0] + piece_ends, piece_ends) if b > a]
+    piece_count = len(pieces)
     me = lax.axis_index("space")
     slot = lax.axis_index("tm")
     near = me + 1 - 2 * (me % 2)
@@ -256,10 +259,12 @@
             {"space": to},
         )
 
-    near_copies = [tau_copy(near, piece, piece) for piece in range(2)]
+    near_copies = [tau_copy(near, piece, 0) for piece in range(2)]
+    near_whole = tau_copy(near, slice(None), 0)
     across_raw = tau_copy(across, slice(None), 6)
-    across_copies = [tau_copy(across, piece, 12 + piece) for piece in range(2)]
-    mirror_copy = tau_copy(mirror, slice(None), 7)
+    across_copies = [tau_copy(across, piece, 11) for piece in range(2)]
+    across_whole = tau_copy(across, slice(None), 11)
+    mirror_copy = tau_copy(mirror, slice(None), 1)
     def early_copy(piece):
         first, count = early_rows[piece]
         return hop(
@@ -268,19 +273,19 @@
             ],
             tau.at[me, :, pl.ds(first, count), pl.ds(0, early_count)],
             send.at[1],
-            recv.at[10 + piece],
+            recv.at[10],
             {"space": mirror},
         )
 
-    lead = vector_count * 5 // 12 // 32 * 32
-    early_rows = [(0, lead), (lead, vector_count - lead)]
-    early_copies = [early_copy(piece) for piece in range(2)]
+    lead = vector_count // 2 // 32 * 32
+    early_rows = [(0, lead), (lead, 32), (lead + 32, vector_count - lead - 32)]
+    early_copies = [early_copy(piece) for piece in range(3)]
     prop_copies = [
         hop(
-            prop_out.at[pl.ds(p * piece_rows, piece_rows), :],
-            prop_in.at[pl.ds(p * piece_rows, piece_rows), :],
+            prop_out.at[pieces[p], :],
+            prop_in.at[pieces[p], :],
             send.at[1],
-            recv.at[14 + p],
+            recv.at[12 + p],
             {"space": mirror},
         )
         for p in range(piece_count)
@@ -442,10 +447,12 @@
             forward(q)
             if q == chunk_count - 1:
                 early_copies[1].start()
+                pl.when(core == 0)(early_copies[2].start)
             if q > 1:
                 settle(q - 2)
         for q in range(chunk_count - 2, chunk_count):
             settle(q)
+        pl.when(core == 1)(early_copies[2].start)
         near_copies[1].start()
         pl.semaphore_wait(ready.at[3], 1)
 
@@ -475,10 +482,6 @@
         res_ref[origin, 0] = product[:, :vector_count]
         res_ref[origin, 1] = product[:, vector_count:]
 
-    def arrived(copies):
-        for copy in copies:
-            copy.wait_recv()
-
     @pl.when(inner == 1)
     def _():
         late_copy.wait()
@@ -502,12 +505,12 @@
 
     @pl.when(inner == 1)
     def _():
-        arrived(near_copies)
+        near_whole.wait_recv()
         left_multiply(near)
 
     @pl.when(inner == 0)
     def _():
-        arrived([across_raw])
+        across_raw.wait_recv()
         left_multiply(across)
 
     chip_hop.wait_recv()
@@ -529,18 +532,19 @@
     @pl.when(inner == 0)
     def _():
         right_multiply(across)
-        for origin, copies in ((near, near_copies), (mirror, [mirror_copy])):
-            arrived(copies)
+        for origin, copy in ((near, near_whole), (mirror, mirror_copy)):
+            copy.wait_recv()
             left_multiply(origin)
             right_multiply(origin)
 
     @pl.when(inner == 1)
     def _():
         right_multiply(near)
-        arrived(across_copies)
+        across_whole.wait_recv()
         left_multiply(across)
         right_multiply(across)
-        arrived(early_copies)
+        landed = tau.at[mirror, :, :, pl.ds(0, early_count)]
+        hop(landed, landed, send.at[1], recv.at[10], {"space": mirror}).wait_recv()
         both = jnp.concatenate(carried(tau[mirror, :, :, :early_count]), axis=1)
         source_early = jnp.concatenate(
             [
@@ -556,7 +560,7 @@
         source_late[late_count:] = source_big[:, vector_count + early_count :].T
 
         def add_piece(p):
-            rows = pl.ds(p * piece_rows, piece_rows)
+            rows = pieces[p]
             prop_copies[p].wait_recv()
             product = block_dot(prop_in[rows, :], source_late[...], 1, 0)
             res_ref[mirror, 0, rows, :] += product[:, :vector_count]
@@ -623,7 +627,7 @@
             pltpu.VMEM((site_count, 128), f32),
             dma((5,)),
             dma((3,)),
-            dma((18,)),
+            dma((16,)),
             dma((3,)),
             pltpu.SemaphoreType.REGULAR((5,)),
         ],

time: 69.8 us -> 69.9 us (level)
  no operation moved by 1% of the time
where the time goes in v4:
time: 69.9 us; the launch traced here: 69.2 us
  Pallas kernels  68.3 us (98%)
  between operations  0.82 us (1%)
    pallas_call x1, Pallas kernels, body(): pl.pallas_call(functools.partial(exchange_kernel, normalizer=normalizer),...  66.2 us
    pallas_call x1, Pallas kernels, body(): pl.pallas_call(finish_kernel, out_shape=jax.ShapeDtypeStruct((1, 2, vecto...  2.19 us

profile of v4, /device:TPU:8, one launch (start us, length us, event | category | flops | bytes accessed | tf_op | source)
XLA Modules:
  0.0 69.2 jit_solution(17626023286400405653)
XLA Ops:
  0.7 66.2 %exchange.1.res_ref = f32[4,2,384,384]{3,2,1,0:T(8,128)S(1)} custom-call(s32[2,3]{1,0:T(2,128)} %momenta_hbm.1, s32[2,2]{1,0:T(2,128)} %ratio_hbm.1, s32[1]{0:T(128)S(6)} %copy.6.slice_ref, bf16[1,2,3,768,384]{4,3,2,1,0:T(8,128)(2,1)} %eig_hbm.1, bf16[1,2,1536,384]{3,2,1,0:T(8,128)(2,1)} %tau_hbm.1), custom_call_target="tpu_custom_call" | custom-call | tf_op jit(solution)/shard_map/exchange/pallas_call | solution.py:606
  66.8 2.2 %finish.1 = f32[1,2,384,1536]{3,2,1,0:T(8,128)} custom-call(f32[4,2,384,384]{3,2,1,0:T(8,128)S(1)} %exchange.1.res_ref), custom_call_target="tpu_custom_call" | custom-call | tf_op jit(solution)/shard_map/finish/pallas_call | solution.py:647

commit v5 on v4

--- a/solution.py
+++ b/solution.py
@@ -160,12 +160,15 @@
 def exchange_kernel(
     momenta_hbm,
     ratio_hbm,
-    slice_ref,
+    slice_hbm,
     eig_hbm,
     tau_hbm,
     res_ref,
+    prop_in,
+    source_late,
     momenta_ref,
     ratio_ref,
+    slice_ref,
     eig,
     acc,
     tau,
@@ -181,10 +184,8 @@
     far,
     sink_big,
     source_big,
-    source_late,
     prop,
     prop_out,
-    prop_in,
     cosines,
     sines,
     own_sem,
@@ -204,7 +205,7 @@
     step_count = color_count * steps_per_color
     late_count = tau_mine.shape[2]
     early_count = vector_count - late_count
-    last_rows = vector_count // 12 // 32 * 32
+    last_rows = tail_rows(vector_count)
     piece_rows = (vector_count - last_rows) // 3 // 32 * 32
     piece_ends = [piece_rows, 2 * piece_rows, vector_count - last_rows, vector_count]
     pieces = [pl.ds(a, b - a) for a, b in zip([0] + piece_ends, piece_ends) if b > a]
@@ -233,6 +234,7 @@
     scalar_copies = [
         pltpu.make_async_copy(momenta_hbm, momenta_ref, own_sem.at[2]),
         pltpu.make_async_copy(ratio_hbm, ratio_ref, own_sem.at[3]),
+        pltpu.make_async_copy(slice_hbm, slice_ref, own_sem.at[5]),
     ]
 
     barrier = pltpu.get_barrier_semaphore()
@@ -278,7 +280,8 @@
         )
 
     lead = vector_count // 2 // 32 * 32
-    early_rows = [(0, lead), (lead, 32), (lead + 32, vector_count - lead - 32)]
+    early_ends = [lead, lead + lead // 3 // 32 * 32, vector_count]
+    early_rows = [(a, b - a) for a, b in zip([0] + early_ends, early_ends)]
     early_copies = [early_copy(piece) for piece in range(3)]
     prop_copies = [
         hop(
@@ -566,8 +569,9 @@
             res_ref[mirror, 0, rows, :] += product[:, :vector_count]
             res_ref[mirror, 1, rows, :] += product[:, vector_count:]
 
-        for p in range(piece_count):
+        for p in range(piece_count - 1):
             add_piece(p)
+        prop_copies[-1].wait_recv()
         hop(sink, sink, send.at[1], recv.at[0], {"space": near}).wait_send()
 
     hop(tau, tau, send.at[0], recv.at[0], {"space": near}).wait_send()
@@ -575,22 +579,46 @@
     hop(tau.at[pair], tau.at[pair], send.at[2], recv.at[0], {"space": near}).wait_send()
 
 
-def finish_kernel(res_ref, out_hbm, sem):
+def finish_kernel(res_ref, prop_ref, source_ref, out_hbm, last, sem):
     group, _, vector_count, _ = res_ref.shape
+    last_rows = last.shape[1]
+    body_rows = pl.ds(0, vector_count - last_rows)
+    tail = pl.ds(vector_count - last_rows, last_rows)
+    me = lax.axis_index("space")
+    mirror = group - 1 - me
+    inner = ((me + 1) // 2) % 2
+
+    def put(source, origin, rows):
+        columns = pl.ds(origin * vector_count, vector_count)
+        pltpu.make_async_copy(source, out_hbm.at[0, :, rows, columns], sem).start()
+
     for origin in range(group):
-        pltpu.make_async_copy(
-            res_ref.at[origin],
-            out_hbm.at[0, :, :, pl.ds(origin * vector_count, vector_count)],
-            sem,
-        ).start()
+        put(res_ref.at[origin, :, body_rows, :], origin, body_rows)
+
+    @pl.when(inner == 1)
+    def _():
+        product = block_dot(prop_ref[tail, :], source_ref[...], 1, 0)
+        last[0] = res_ref[mirror, 0, tail, :] + product[:, :vector_count]
+        last[1] = res_ref[mirror, 1, tail, :] + product[:, vector_count:]
+
+    for origin in range(group):
+        late = jnp.logical_and(inner == 1, mirror == origin)
+        pl.when(late)(functools.partial(put, last, origin, tail))
+        pl.when(jnp.logical_not(late))(
+            functools.partial(put, res_ref.at[origin, :, tail, :], origin, tail)
+        )
     pltpu.make_async_copy(res_ref, res_ref, sem).wait()
+
+
+def tail_rows(vector_count):
+    return vector_count // 12 // 32 * 32
 
 
 def in_hbm(array):
     return pltpu.with_memory_space_constraint(array, pltpu.HBM)
 
 
-def body(eigenvectors, perambulator, momenta, ratios, source_slice):
+def both_kernels(eigenvectors, perambulator, momenta, ratios, source_slice):
     color_count, site_count, vector_count = eigenvectors.shape[2:]
     group = lax.axis_size("space")
     normalizer = 1.0 / math.sqrt(color_count * site_count * group * vector_count)
@@ -598,19 +626,23 @@
     late_count = 128
     whole = (chunk_count, 2, vector_count // chunk_count, vector_count)
     bf16, f32 = jnp.bfloat16, jnp.float32
-    smem = pl.BlockSpec(memory_space=pltpu.SMEM)
     vmem = pl.BlockSpec(memory_space=pltpu.VMEM)
     anywhere = pl.BlockSpec(memory_space=pl.ANY)
     dma = pltpu.SemaphoreType.DMA
     room = 4 * group * 2 * vector_count * vector_count
-    result = pl.pallas_call(
+    results = pl.pallas_call(
         functools.partial(exchange_kernel, normalizer=normalizer),
-        out_shape=pltpu.VMEM((group, 2, vector_count, vector_count), f32),
-        in_specs=[anywhere, anywhere, smem, anywhere, anywhere],
-        out_specs=vmem,
+        out_shape=(
+            pltpu.VMEM((group, 2, vector_count, vector_count), f32),
+            pltpu.VMEM((vector_count, 2 * late_count), bf16),
+            pltpu.VMEM((2 * late_count, 2 * vector_count), bf16),
+        ),
+        in_specs=[anywhere] * 5,
+        out_specs=(vmem, vmem, vmem),
         scratch_shapes=[
             pltpu.SMEM(momenta.shape, jnp.int32),
             pltpu.SMEM(ratios.shape, jnp.int32),
+            pltpu.SMEM(source_slice.shape, jnp.int32),
             pltpu.VMEM(eigenvectors.shape[1:], bf16),
             pltpu.VMEM((vector_count, 4 * vector_count), f32),
             pltpu.VMEM((group, 2, vector_count, vector_count), bf16),
@@ -619,13 +651,11 @@
             *[pltpu.VMEM(whole, bf16) for _ in range(8)],
             pltpu.VMEM((2 * vector_count, 2 * vector_count), bf16),
             pltpu.VMEM((2 * vector_count, 2 * vector_count), bf16),
-            pltpu.VMEM((2 * late_count, 2 * vector_count), bf16),
             pltpu.VMEM((group, vector_count, 2 * vector_count), bf16),
-            pltpu.VMEM((vector_count, 2 * late_count), bf16),
             pltpu.VMEM((vector_count, 2 * late_count), bf16),
             pltpu.VMEM((site_count, 128), f32),
             pltpu.VMEM((site_count, 128), f32),
-            dma((5,)),
+            dma((6,)),
             dma((3,)),
             dma((16,)),
             dma((3,)),
@@ -640,19 +670,30 @@
     )(
         in_hbm(momenta),
         in_hbm(ratios),
-        source_slice,
+        in_hbm(source_slice),
         in_hbm(eigenvectors),
         in_hbm(perambulator),
     )
     return pl.pallas_call(
         finish_kernel,
-        out_shape=jax.ShapeDtypeStruct((1, 2, vector_count, group * vector_count), f32),
-        in_specs=[vmem],
+        out_shape=pltpu.HBM((1, 2, vector_count, group * vector_count), f32),
+        in_specs=[vmem, vmem, vmem],
         out_specs=anywhere,
-        scratch_shapes=[dma],
+        scratch_shapes=[pltpu.VMEM((2, tail_rows(vector_count), vector_count), f32), dma],
         compiler_params=pltpu.CompilerParams(vmem_limit_bytes=VMEM_BYTES // 2),
         name="finish",
-    )(pltpu.with_memory_space_constraint(result, pltpu.VMEM))
+    )(*[pltpu.with_memory_space_constraint(array, pltpu.VMEM) for array in results])
+
+
+def body(*arrays):
+    perambulator = arrays[1]
+    group = lax.axis_size("space")
+    part_count, order, columns = perambulator.shape[1:]
+
+    def never(*_):
+        return jnp.zeros((1, part_count, order // group, columns * group), jnp.float32)
+
+    return lax.cond(lax.axis_index("space") < 2 * group, both_kernels, never, *arrays)
 
 
 def fits(mesh, eigenvectors, perambulator):
@@ -664,7 +705,7 @@
         and eigenvectors.shape[0] == slots * mesh.shape["cfg"]
         and perambulator.shape[2] == space * vector_count
         and vector_count % 128 == 0
-        and vector_count > 128
+        and vector_count >= 384
         and eigenvectors.shape[3] % (32 * space) == 0
     )
 

time: 69.9 us -> 69.7 us (level)
  no operation moved by 1% of the time
where the time goes in v5:
time: 69.7 us; the launch traced here: 69 us
  Pallas kernels  68.8 us (99%)
    pallas_call x1, Pallas kernels, both_kernels(): pl.pallas_call(functools.partial(exchange_kernel, normalizer=normalizer),...  66.6 us
    pallas_call x1, Pallas kernels, both_kernels(): pl.pallas_call(finish_kernel, out_shape=pltpu.HBM((1, 2, vector_count, gr...  2.17 us

profile of v5, /device:TPU:8, one launch (start us, length us, event | category | flops | bytes accessed | tf_op | source)
XLA Modules:
  0.0 69.0 jit_solution(923289096272967455)
XLA Ops:
  0.0 68.8 %conditional.1 = (f32[1,2,384,1536]{3,2,1,0:T(8,128)}) conditional(s32[]{:T(128)} %convert_element_type.3, () %tuple.11, (s32[2,3]{1,0:T(2,128)}, s32[2,2]{1,0:T(2,128)}, s32[1]{0:T(128)}, bf16[1,2,3,768,384]{4,3,2,1,0:T(8,128)(2,1)}, bf16[1,2,1536,384]{3,2,1,0:T(8,128)(2,1)}) %tuple.12), branch_computations={%region_0.0_spmd, %region_1.0_spmd} | conditional | bytes 4718604 | solution.py:696
  0.0 66.6 %exchange.1 = (f32[4,2,384,384]{3,2,1,0:T(8,128)S(1)}, bf16[384,256]{1,0:T(8,128)(2,1)S(1)}, bf16[256,768]{1,0:T(8,128)(2,1)S(1)}) custom-call(s32[2,3]{1,0:T(2,128)} %get-tuple-element.32.momenta_hbm, s32[2,2]{1,0:T(2,128)} %get-tuple-element.33.ratio_hbm, s32[1]{0:T(128)} %get-tuple-element.34.slice_hbm, ...), custom_call_target="tpu_custom_call" | custom-call | tf_op jit(solution)/shard_map/cond/branch_1_fun/exchange/pallas_call | solution.py:633
  66.7 2.2 %finish.1 = f32[1,2,384,1536]{3,2,1,0:T(8,128)} custom-call(f32[4,2,384,384]{3,2,1,0:T(8,128)S(1)} %get-tuple-element.23.res_ref, bf16[384,256]{1,0:T(8,128)(2,1)S(1)} %get-tuple-element.24.prop_ref, bf16[256,768]{1,0:T(8,128)(2,1)S(1)} %get-tuple-element.25.source_ref), custom_call_target="tpu_custom_call" | custom-call | tf_op jit(solution)/shard_map/cond/branch_1_fun/finish/pallas_call | solution.py:677

commit v6 on v5

--- a/solution.py
+++ b/solution.py
@@ -280,9 +280,14 @@
         )
 
     lead = vector_count // 2 // 32 * 32
-    early_ends = [lead, lead + lead // 3 // 32 * 32, vector_count]
+    early_ends = [
+        lead,
+        lead + lead // 4 // 16 * 16,
+        lead + lead // 2 // 16 * 16,
+        vector_count,
+    ]
     early_rows = [(a, b - a) for a, b in zip([0] + early_ends, early_ends)]
-    early_copies = [early_copy(piece) for piece in range(3)]
+    early_copies = [early_copy(piece) for piece in range(4)]
     prop_copies = [
         hop(
             prop_out.at[pieces[p], :],
@@ -435,6 +440,8 @@
             for c in range(2):
                 part[q, c] = weighted(q, c)
 
+        first_half = jnp.logical_or(core == 0, me // 2 == 1)
+
         def forward(q):
             pair_hops[q].wait_recv()
             part[q] = part[q] + pair_in[q].astype(jnp.float32)
@@ -450,12 +457,14 @@
             forward(q)
             if q == chunk_count - 1:
                 early_copies[1].start()
-                pl.when(core == 0)(early_copies[2].start)
+                pl.when(first_half)(early_copies[2].start)
+                pl.when(core == 0)(early_copies[3].start)
             if q > 1:
                 settle(q - 2)
         for q in range(chunk_count - 2, chunk_count):
             settle(q)
-        pl.when(core == 1)(early_copies[2].start)
+        pl.when(jnp.logical_not(first_half))(early_copies[2].start)
+        pl.when(core == 1)(early_copies[3].start)
         near_copies[1].start()
         pl.semaphore_wait(ready.at[3], 1)
 

time: 69.7 us -> 69.5 us (level)
  no operation moved by 1% of the time
where the time goes in v6:
time: 69.5 us; the launch traced here: 69.3 us
  Pallas kernels  69.2 us (100%)
    pallas_call x1, Pallas kernels, both_kernels(): pl.pallas_call(functools.partial(exchange_kernel, normalizer=normalizer),...  67 us
    pallas_call x1, Pallas kernels, both_kernels(): pl.pallas_call(finish_kernel, out_shape=pltpu.HBM((1, 2, vector_count, gr...  2.17 us

profile of v6, /device:TPU:8, one launch (start us, length us, event | category | flops | bytes accessed | tf_op | source)
XLA Modules:
  0.0 69.3 jit_solution(3588502391241154512)
XLA Ops:
  0.0 69.2 %conditional.1 = (f32[1,2,384,1536]{3,2,1,0:T(8,128)}) conditional(s32[]{:T(128)} %convert_element_type.3, () %tuple.11, (s32[2,3]{1,0:T(2,128)}, s32[2,2]{1,0:T(2,128)}, s32[1]{0:T(128)}, bf16[1,2,3,768,384]{4,3,2,1,0:T(8,128)(2,1)}, bf16[1,2,1536,384]{3,2,1,0:T(8,128)(2,1)}) %tuple.12), branch_computations={%region_0.0_spmd, %region_1.0_spmd} | conditional | bytes 4718604 | solution.py:705
  0.0 67.0 %exchange.1 = (f32[4,2,384,384]{3,2,1,0:T(8,128)S(1)}, bf16[384,256]{1,0:T(8,128)(2,1)S(1)}, bf16[256,768]{1,0:T(8,128)(2,1)S(1)}) custom-call(s32[2,3]{1,0:T(2,128)} %get-tuple-element.32.momenta_hbm, s32[2,2]{1,0:T(2,128)} %get-tuple-element.33.ratio_hbm, s32[1]{0:T(128)} %get-tuple-element.34.slice_hbm, ...), custom_call_target="tpu_custom_call" | custom-call | tf_op jit(solution)/shard_map/cond/branch_1_fun/exchange/pallas_call | solution.py:642
  67.0 2.2 %finish.1 = f32[1,2,384,1536]{3,2,1,0:T(8,128)} custom-call(f32[4,2,384,384]{3,2,1,0:T(8,128)S(1)} %get-tuple-element.23.res_ref, bf16[384,256]{1,0:T(8,128)(2,1)S(1)} %get-tuple-element.24.prop_ref, bf16[256,768]{1,0:T(8,128)(2,1)S(1)} %get-tuple-element.25.source_ref), custom_call_target="tpu_custom_call" | custom-call | tf_op jit(solution)/shard_map/cond/branch_1_fun/finish/pallas_call | solution.py:686

commit v7 on v6

--- a/solution.py
+++ b/solution.py
@@ -205,8 +205,8 @@
     step_count = color_count * steps_per_color
     late_count = tau_mine.shape[2]
     early_count = vector_count - late_count
-    last_rows = tail_rows(vector_count)
-    piece_rows = (vector_count - last_rows) // 3 // 32 * 32
+    last_rows = vector_count // 12 // 32 * 32
+    piece_rows = (vector_count - tail_rows(vector_count)) // 2
     piece_ends = [piece_rows, 2 * piece_rows, vector_count - last_rows, vector_count]
     pieces = [pl.ds(a, b - a) for a, b in zip([0] + piece_ends, piece_ends) if b > a]
     piece_count = len(pieces)
@@ -578,9 +578,10 @@
             res_ref[mirror, 0, rows, :] += product[:, :vector_count]
             res_ref[mirror, 1, rows, :] += product[:, vector_count:]
 
-        for p in range(piece_count - 1):
+        for p in range(piece_count - 2):
             add_piece(p)
-        prop_copies[-1].wait_recv()
+        for copy in prop_copies[piece_count - 2 :]:
+            copy.wait_recv()
         hop(sink, sink, send.at[1], recv.at[0], {"space": near}).wait_send()
 
     hop(tau, tau, send.at[0], recv.at[0], {"space": near}).wait_send()
@@ -604,6 +605,10 @@
     for origin in range(group):
         put(res_ref.at[origin, :, body_rows, :], origin, body_rows)
 
+    for origin in range(group):
+        kept = jnp.logical_or(inner == 0, mirror != origin)
+        pl.when(kept)(functools.partial(put, res_ref.at[origin, :, tail, :], origin, tail))
+
     @pl.when(inner == 1)
     def _():
         product = block_dot(prop_ref[tail, :], source_ref[...], 1, 0)
@@ -613,14 +618,13 @@
     for origin in range(group):
         late = jnp.logical_and(inner == 1, mirror == origin)
         pl.when(late)(functools.partial(put, last, origin, tail))
-        pl.when(jnp.logical_not(late))(
-            functools.partial(put, res_ref.at[origin, :, tail, :], origin, tail)
-        )
+
     pltpu.make_async_copy(res_ref, res_ref, sem).wait()
 
 
 def tail_rows(vector_count):
-    return vector_count // 12 // 32 * 32
+    last_rows = vector_count // 12 // 32 * 32
+    return vector_count - (vector_count - last_rows) // 3 // 32 * 64
 
 
 def in_hbm(array):

time: 69.5 us -> 69.4 us (level)
  no operation moved by 1% of the time
where the time goes in v7:
time: 69.4 us; the launch traced here: 69.2 us
  Pallas kernels  69.1 us (100%)
    pallas_call x1, Pallas kernels, both_kernels(): pl.pallas_call(functools.partial(exchange_kernel, normalizer=normalizer),...  66.9 us
    pallas_call x1, Pallas kernels, both_kernels(): pl.pallas_call(finish_kernel, out_shape=pltpu.HBM((1, 2, vector_count, gr...  2.19 us

profile of v7, /device:TPU:8, one launch (start us, length us, event | category | flops | bytes accessed | tf_op | source)
XLA Modules:
  0.0 69.2 jit_solution(17889013889320904593)
XLA Ops:
  0.0 69.1 %conditional.1 = (f32[1,2,384,1536]{3,2,1,0:T(8,128)}) conditional(s32[]{:T(128)} %convert_element_type.3, () %tuple.11, (s32[2,3]{1,0:T(2,128)}, s32[2,2]{1,0:T(2,128)}, s32[1]{0:T(128)}, bf16[1,2,3,768,384]{4,3,2,1,0:T(8,128)(2,1)}, bf16[1,2,1536,384]{3,2,1,0:T(8,128)(2,1)}) %tuple.12), branch_computations={%region_0.0_spmd, %region_1.0_spmd} | conditional | bytes 4718604 | solution.py:709
  0.0 66.9 %exchange.1 = (f32[4,2,384,384]{3,2,1,0:T(8,128)S(1)}, bf16[384,256]{1,0:T(8,128)(2,1)S(1)}, bf16[256,768]{1,0:T(8,128)(2,1)S(1)}) custom-call(s32[2,3]{1,0:T(2,128)} %get-tuple-element.32.momenta_hbm, s32[2,2]{1,0:T(2,128)} %get-tuple-element.33.ratio_hbm, s32[1]{0:T(128)} %get-tuple-element.34.slice_hbm, ...), custom_call_target="tpu_custom_call" | custom-call | tf_op jit(solution)/shard_map/cond/branch_1_fun/exchange/pallas_call | solution.py:646
  66.9 2.2 %finish.1 = f32[1,2,384,1536]{3,2,1,0:T(8,128)} custom-call(f32[4,2,384,384]{3,2,1,0:T(8,128)S(1)} %get-tuple-element.23.res_ref, bf16[384,256]{1,0:T(8,128)(2,1)S(1)} %get-tuple-element.24.prop_ref, bf16[256,768]{1,0:T(8,128)(2,1)S(1)} %get-tuple-element.25.source_ref), custom_call_target="tpu_custom_call" | custom-call | tf_op jit(solution)/shard_map/cond/branch_1_fun/finish/pallas_call | solution.py:690

commit v8 on v6

--- a/solution.py
+++ b/solution.py
@@ -264,8 +264,8 @@
     near_copies = [tau_copy(near, piece, 0) for piece in range(2)]
     near_whole = tau_copy(near, slice(None), 0)
     across_raw = tau_copy(across, slice(None), 6)
-    across_copies = [tau_copy(across, piece, 11) for piece in range(2)]
-    across_whole = tau_copy(across, slice(None), 11)
+    across_copies = [tau_copy(across, piece, 10) for piece in range(2)]
+    across_whole = tau_copy(across, slice(None), 10)
     mirror_copy = tau_copy(mirror, slice(None), 1)
     def early_copy(piece):
         first, count = early_rows[piece]
@@ -275,7 +275,7 @@
             ],
             tau.at[me, :, pl.ds(first, count), pl.ds(0, early_count)],
             send.at[1],
-            recv.at[10],
+            recv.at[1],
             {"space": mirror},
         )
 
@@ -293,7 +293,7 @@
             prop_out.at[pieces[p], :],
             prop_in.at[pieces[p], :],
             send.at[1],
-            recv.at[12 + p],
+            recv.at[11 + p],
             {"space": mirror},
         )
         for p in range(piece_count)
@@ -354,7 +354,7 @@
         phases()
         pl.semaphore_wait(ready.at[0], 1)
         pl.semaphore_wait(ready.at[1], 1)
-        tell(3, {"space": near})
+        tell(2, {"space": near})
 
     own_copy.start()
 
@@ -426,8 +426,8 @@
         pl.semaphore_wait(ready.at[2], 1)
         for q in range(chunk_count // 2):
             back_hops[q].wait_recv()
-        tell(4, {"tm": core_peer})
-        pl.semaphore_wait(ready.at[4], 1)
+        tell(3, {"tm": core_peer})
+        pl.semaphore_wait(ready.at[3], 1)
         across_copies[0].start()
         mirror_copy.start()
         across_copies[1].start()
@@ -466,7 +466,7 @@
         pl.when(jnp.logical_not(first_half))(early_copies[2].start)
         pl.when(core == 1)(early_copies[3].start)
         near_copies[1].start()
-        pl.semaphore_wait(ready.at[3], 1)
+        pl.semaphore_wait(ready.at[2], 1)
 
     core_hop = hop(sink, sink_pair, send.at[2], spread_recv.at[0], {"tm": core_peer})
     core_hop.start()
@@ -556,7 +556,7 @@
         left_multiply(across)
         right_multiply(across)
         landed = tau.at[mirror, :, :, pl.ds(0, early_count)]
-        hop(landed, landed, send.at[1], recv.at[10], {"space": mirror}).wait_recv()
+        hop(landed, landed, send.at[1], recv.at[1], {"space": mirror}).wait_recv()
         both = jnp.concatenate(carried(tau[mirror, :, :, :early_count]), axis=1)
         source_early = jnp.concatenate(
             [
@@ -666,9 +666,9 @@
             pltpu.VMEM((site_count, 128), f32),
             dma((6,)),
             dma((3,)),
-            dma((16,)),
+            dma((15,)),
             dma((3,)),
-            pltpu.SemaphoreType.REGULAR((5,)),
+            pltpu.SemaphoreType.REGULAR((4,)),
         ],
         compiler_params=pltpu.CompilerParams(
             collective_id=0,

time: 69.5 us -> 69.5 us (level)
  no operation moved by 1% of the time
where the time goes in v8:
time: 69.5 us; the launch traced here: 69.3 us
  Pallas kernels  69.1 us (99%)
    pallas_call x1, Pallas kernels, both_kernels(): pl.pallas_call(functools.partial(exchange_kernel, normalizer=normalizer),...  67 us
    pallas_call x1, Pallas kernels, both_kernels(): pl.pallas_call(finish_kernel, out_shape=pltpu.HBM((1, 2, vector_count, gr...  2.17 us

profile of v8, /device:TPU:8, one launch (start us, length us, event | category | flops | bytes accessed | tf_op | source)
XLA Modules:
  0.0 69.3 jit_solution(13601779431008260050)
XLA Ops:
  0.0 69.1 %conditional.1 = (f32[1,2,384,1536]{3,2,1,0:T(8,128)}) conditional(s32[]{:T(128)} %convert_element_type.3, () %tuple.11, (s32[2,3]{1,0:T(2,128)}, s32[2,2]{1,0:T(2,128)}, s32[1]{0:T(128)}, bf16[1,2,3,768,384]{4,3,2,1,0:T(8,128)(2,1)}, bf16[1,2,1536,384]{3,2,1,0:T(8,128)(2,1)}) %tuple.12), branch_computations={%region_0.0_spmd, %region_1.0_spmd} | conditional | bytes 4718604 | solution.py:705
  0.0 67.0 %exchange.1 = (f32[4,2,384,384]{3,2,1,0:T(8,128)S(1)}, bf16[384,256]{1,0:T(8,128)(2,1)S(1)}, bf16[256,768]{1,0:T(8,128)(2,1)S(1)}) custom-call(s32[2,3]{1,0:T(2,128)} %get-tuple-element.32.momenta_hbm, s32[2,2]{1,0:T(2,128)} %get-tuple-element.33.ratio_hbm, s32[1]{0:T(128)} %get-tuple-element.34.slice_hbm, ...), custom_call_target="tpu_custom_call" | custom-call | tf_op jit(solution)/shard_map/cond/branch_1_fun/exchange/pallas_call | solution.py:642
  67.0 2.2 %finish.1 = f32[1,2,384,1536]{3,2,1,0:T(8,128)} custom-call(f32[4,2,384,384]{3,2,1,0:T(8,128)S(1)} %get-tuple-element.23.res_ref, bf16[384,256]{1,0:T(8,128)(2,1)S(1)} %get-tuple-element.24.prop_ref, bf16[256,768]{1,0:T(8,128)(2,1)S(1)} %get-tuple-element.25.source_ref), custom_call_target="tpu_custom_call" | custom-call | tf_op jit(solution)/shard_map/cond/branch_1_fun/finish/pallas_call | solution.py:686
